TPU v7x, 32 devices: a whole 2x2x4 slice. The times are simulated.
32 devices in a mesh: groups: 2 (over y), gz: 4 (over z), dev: 2 (over x), xy: 2 (over core).
Axes of the slice: x: 2, y: 2, z: 4, core: 2. Of those that a mesh axis runs over, the one named last changes fastest.
Arguments:
- fields: float32 [12, 8, 64, 256], P('groups', 'dev', 'gz', 'xy'), parts along dimension 0, may hold values from -6 to 6
- spectra: float32 [24, 8, 64, 256], P('groups', 'dev', 'gz', 'xy'), parts along dimension 0, may hold values from -6 to 6
- permittivity: float32 [16, 64, 256], P(('groups', 'dev'), 'gz', 'xy'), parts along dimension 0, may hold values from 1 to 12
- phase_start: float32 [2], P('groups'), parts along dimension 0, may hold values from -3.140625 to 3.140625
- wall_owner: int32 [4, 4], P('gz'), may hold values from 0 to 3, as said below
- cap_owner: int32 [2, 32], replicated, may hold values from 0 to 3, as said below
- dir_index: int32 [2048], replicated, may hold values from 0 to 4095
- target: float32 [4096], P('groups'), parts along dimension 0, may hold values from 1 to 12
- aim_mask: int32 [4096], P('groups'), parts along dimension 0, may hold values 0 or 1
Outputs:
- fields_out: float32 [12, 8, 64, 256], P('groups', 'dev', 'gz', 'xy'), parts along dimension 0
- spectra_out: float32 [24, 8, 64, 256], P('groups', 'dev', 'gz', 'xy'), parts along dimension 0
- owned_currents: float32 [8, 2, 2, 20, 128], P(('groups', 'gz'), 'dev', 'xy'), parts along dimension 0
- intensity: float32 [4096], P(('groups', 'gz', 'dev', 'xy')), parts along dimension 0
- adjoint_currents: float32 [8, 2, 2, 36, 128], P(('groups', 'gz'), 'dev', 'xy'), parts along dimension 0
There are 2 independent parts, one for each index of `groups`. A program takes and returns all parts, laid end to end along the dimension named above; an argument that names none is the same for every part. Nothing has to cross between parts.
Inputs may be any that keep to these rules, and one draw needn't show every extreme that they name: `wall_owner`: entry [s, j] names the index of gz that owns wall patch j of slab s; every index owns exactly 4 wall patches of a column, and a slab gives one index at most 1 of them. `cap_owner`: row 0 names the owner on gz of each patch of the lower cap, row 1 of the upper cap; each index owns exactly 8 patches of each cap, so that every index owns exactly 20 patches of a column.
All inputs are finite; a program needn't handle non-finite values.
Results may differ from a plain program's by a relative error of at most 0.0003.
Values sent between devices are 32-bit elements; how exact they have to be, the bound alone decides.
A program may use at most 64 MiB of HBM per device.

v0:
```python
import math

import jax
import jax.numpy as jnp
from jax import lax
from jax.sharding import PartitionSpec as P

PATCH = 16
XB = 8
ZB = 4
STEPS = 3
THETAS = 64


COURANT = 0.5
ANGULAR_STEP = 0.3
WAVE_NUMBER = 0.6
HIGHEST = lax.Precision.HIGHEST
CURRENT_SIGNS = (-1.0, 1.0, 1.0, -1.0)
X_PICKS = (5, 4, 2, 1)
Z_PICKS = (4, 3, 1, 0)


def padded_2(shard, sides, width):
    for axis, dim in sides:
        peers, length = (lax.axis_size(axis), shard.shape[dim])
        up = [(i, (i + 1) % peers) for i in range(peers - 1)]
        down = [(j, i) for i, j in up]
        last = lax.slice_in_dim(shard, length - width, length, axis=dim)
        first = lax.slice_in_dim(shard, 0, width, axis=dim)
        before = lax.ppermute(last, axis, up)
        after = lax.ppermute(first, axis, down)
        shard = jnp.concatenate([before, shard, after], axis=dim)
    return shard


def broadcast(block, axis, holder):
    block = jnp.where(lax.axis_index(axis) == holder, block, jnp.zeros_like(block))
    return lax.psum(block, axis)


def spectral_update(spectra_now, electric, magnetic, phase_start, step_number):
    angle_half = phase_start[0] + ANGULAR_STEP * (step_number + 0.5)
    angle_full = phase_start[0] + ANGULAR_STEP * (step_number + 1.0)
    return jnp.concatenate(
        [
            spectra_now[0:3] + electric * jnp.cos(angle_full),
            spectra_now[3:6] + magnetic * jnp.cos(angle_half),
            spectra_now[6:9] - electric * jnp.sin(angle_full),
            spectra_now[9:12] - magnetic * jnp.sin(angle_half),
        ]
    )


def face_values(spectral_plane, facing, chosen):
    real_part = [
        CURRENT_SIGNS[number] * facing * spectral_plane[chosen[number]] for number in range(4)
    ]
    imag_part = [
        CURRENT_SIGNS[number] * facing * spectral_plane[6 + chosen[number]] for number in range(4)
    ]
    return jnp.stack(real_part + imag_part)


def to_vectors(record_values, x_flag):
    z_flag = 1.0 - x_flag
    stacked_rows = []
    for offset in (0, 4):
        tangent_one = record_values[offset]
        tangent_two = record_values[offset + 1]
        moment_one = record_values[offset + 2]
        moment_two = record_values[offset + 3]
        stacked_rows += [
            z_flag * tangent_one,
            x_flag * tangent_one + z_flag * tangent_two,
            x_flag * tangent_two,
            z_flag * moment_one,
            x_flag * moment_one + z_flag * moment_two,
            x_flag * moment_two,
        ]
    return jnp.stack(stacked_rows)


def to_record(gradient, x_flag):
    z_flag = 1.0 - x_flag
    stacked_rows = []
    for offset in (0, 6):
        stacked_rows += [
            x_flag * gradient[offset + 1] + z_flag * gradient[offset],
            x_flag * gradient[offset + 2] + z_flag * gradient[offset + 1],
            x_flag * gradient[offset + 4] + z_flag * gradient[offset + 3],
            x_flag * gradient[offset + 5] + z_flag * gradient[offset + 4],
        ]
    return jnp.stack(stacked_rows)


def direction_frames(dir_index):
    polar_row = (dir_index // THETAS).astype(jnp.float32)
    azimuth_col = (dir_index % THETAS).astype(jnp.float32)
    polar_angle = jnp.pi * (polar_row + 0.5) / THETAS
    azimuth = 2.0 * jnp.pi * azimuth_col / THETAS
    sin_polar = jnp.sin(polar_angle)
    cos_polar = jnp.cos(polar_angle)
    sin_azim = jnp.sin(azimuth)
    cos_azim = jnp.cos(azimuth)
    unit_vectors = jnp.stack([sin_polar * cos_azim, sin_polar * sin_azim, cos_polar], axis=1)
    theta_hat = jnp.stack([cos_polar * cos_azim, cos_polar * sin_azim, -sin_polar], axis=1)
    phi_hat = jnp.stack([-sin_azim, cos_azim, jnp.zeros_like(sin_azim)], axis=1)
    return (unit_vectors, theta_hat, phi_hat)


def steering(unit_block, positions):
    angle_table = WAVE_NUMBER * (
        positions[0][:, None] * unit_block[None, :, 0]
        + positions[1][:, None] * unit_block[None, :, 1]
        + positions[2][:, None] * unit_block[None, :, 2]
    )
    return (jnp.cos(angle_table), jnp.sin(angle_table))


def far_block(unit_block, currents, positions):
    cosine_table, sine_table = steering(unit_block, positions)
    real_part = jnp.dot(currents[:6], cosine_table, precision=HIGHEST) - jnp.dot(
        currents[6:], sine_table, precision=HIGHEST
    )
    imag_part = jnp.dot(currents[:6], sine_table, precision=HIGHEST) + jnp.dot(
        currents[6:], cosine_table, precision=HIGHEST
    )
    return jnp.concatenate([real_part, imag_part], axis=0)


def adjoint_block(unit_block, slope_block, positions):
    cosine_table, sine_table = steering(unit_block, positions)
    real_part = jnp.dot(slope_block[:6], cosine_table.T, precision=HIGHEST) + jnp.dot(
        slope_block[6:], sine_table.T, precision=HIGHEST
    )
    imag_part = jnp.dot(slope_block[6:], cosine_table.T, precision=HIGHEST) - jnp.dot(
        slope_block[:6], sine_table.T, precision=HIGHEST
    )
    return jnp.concatenate([real_part, imag_part], axis=0)


def intensity_and_slope(far_total, theta_hat, phi_hat, target, aim_mask):
    theta_rows = theta_hat.T
    phi_rows = phi_hat.T

    def project(vectors, frame_rows):
        return jnp.sum(vectors * frame_rows, axis=0)

    e_theta_re = -(project(far_total[3:6], phi_rows) + project(far_total[0:3], theta_rows))
    e_phi_re = project(far_total[3:6], theta_rows) - project(far_total[0:3], phi_rows)
    e_theta_im = -(project(far_total[9:12], phi_rows) + project(far_total[6:9], theta_rows))
    e_phi_im = project(far_total[9:12], theta_rows) - project(far_total[6:9], phi_rows)
    intensity = (
        e_theta_re * e_theta_re
        + e_theta_im * e_theta_im
        + e_phi_re * e_phi_re
        + e_phi_im * e_phi_im
    )
    residual = aim_mask.astype(jnp.float32) * (intensity - target)
    slope_theta_re = 2.0 * residual * e_theta_re
    slope_phi_re = 2.0 * residual * e_phi_re
    slope_theta_im = 2.0 * residual * e_theta_im
    slope_phi_im = 2.0 * residual * e_phi_im
    n_re = -slope_theta_re * theta_rows - slope_phi_re * phi_rows
    l_re = -slope_theta_re * phi_rows + slope_phi_re * theta_rows
    n_im = -slope_theta_im * theta_rows - slope_phi_im * phi_rows
    l_im = -slope_theta_im * phi_rows + slope_phi_im * theta_rows
    return (intensity, jnp.concatenate([n_re, l_re, n_im, l_im], axis=0))


def rim_keep_mask(length, device_index):
    indices = jnp.arange(length)
    return jnp.where((indices == 0) & (device_index == 0), 0.0, 1.0).astype(jnp.float32)


def yee_step(field_state, step_rate, rim_keep):
    padded = padded_2(field_state, (("gz", 2), ("dev", 1), ("xy", 3)), 1)
    size_y, size_z, size_x = (field_state.shape[1], field_state.shape[2], field_state.shape[3])

    def region(component, shift_y, shift_z, shift_x):
        return padded[
            component,
            shift_y : shift_y + size_y + 1,
            shift_z : shift_z + size_z + 1,
            shift_x : shift_x + size_x + 1,
        ]

    def ahead_diff(component, axis_number):
        shifts = [0, 0, 0]
        shifts[axis_number] = 1
        return region(component, shifts[0], shifts[1], shifts[2]) - region(component, 0, 0, 0)

    magn_x = (region(3, 0, 0, 0) - COURANT * (ahead_diff(2, 0) - ahead_diff(1, 1))) * rim_keep
    magn_y = (region(4, 0, 0, 0) - COURANT * (ahead_diff(0, 1) - ahead_diff(2, 2))) * rim_keep
    magn_z = (region(5, 0, 0, 0) - COURANT * (ahead_diff(1, 2) - ahead_diff(0, 0))) * rim_keep

    def behind(magnetic, axis_number):
        center = magnetic[1:, 1:, 1:]
        if axis_number == 0:
            earlier = magnetic[:-1, 1:, 1:]
        elif axis_number == 1:
            earlier = magnetic[1:, :-1, 1:]
        else:
            earlier = magnetic[1:, 1:, :-1]
        return center - earlier

    elec_x = padded[0, 1:-1, 1:-1, 1:-1] + step_rate * (behind(magn_z, 0) - behind(magn_y, 1))
    elec_y = padded[1, 1:-1, 1:-1, 1:-1] + step_rate * (behind(magn_x, 1) - behind(magn_z, 2))
    elec_z = padded[2, 1:-1, 1:-1, 1:-1] + step_rate * (behind(magn_y, 2) - behind(magn_x, 0))
    electric = jnp.stack([elec_x, elec_y, elec_z])
    magnetic = jnp.stack([magn_x[1:, 1:, 1:], magn_y[1:, 1:, 1:], magn_z[1:, 1:, 1:]])
    return (electric, magnetic)


def point_layout(home_records, home_meta, centers, norm_scale):
    record_total = home_records.shape[0]
    record_values = (
        home_records.reshape(record_total, 8, PATCH)
        .transpose(1, 0, 2)
        .reshape(8, record_total * PATCH)
    )
    x_flag = jnp.repeat(jnp.where(home_meta[:, 3] < 2.5, 1.0, 0.0).astype(jnp.float32), PATCH)
    offsets = jnp.tile(jnp.arange(PATCH, dtype=jnp.float32), record_total)
    positions = jnp.stack(
        [
            jnp.repeat(home_meta[:, 0], PATCH) + offsets * (1.0 - x_flag) - centers[0],
            jnp.repeat(home_meta[:, 1], PATCH) - centers[1],
            jnp.repeat(home_meta[:, 2], PATCH) + offsets * x_flag - centers[2],
        ]
    )
    return (to_vectors(record_values, x_flag) * norm_scale, positions, x_flag)


def cap_layout(cap_count, size_x, size_y, xy_index, dev_index, z_global, flag_value):
    cap_flat = jnp.arange(cap_count, dtype=jnp.int32) * PATCH
    cap_ones = jnp.ones((cap_count,), jnp.float32)
    return jnp.stack(
        [
            (xy_index * size_x + cap_flat % size_x).astype(jnp.float32),
            (dev_index * size_y + cap_flat // size_x).astype(jnp.float32),
            cap_ones * z_global,
            cap_ones * flag_value,
        ],
        axis=1,
    )


def mine_selector(owner_row, gz_index, share):
    mine = owner_row == gz_index
    rank = jnp.cumsum(mine.astype(jnp.int32)) - 1
    return jnp.where(
        (jnp.arange(share, dtype=jnp.int32)[:, None] == rank[None, :]) & mine[None, :], 1.0, 0.0
    ).astype(jnp.float32)


def local(
    fields, spectra, permittivity, phase_start, wall_owner, cap_owner, dir_index, target, aim_mask
):
    slab_count = lax.axis_size("gz")
    dev_count = lax.axis_size("dev")
    xy_count = lax.axis_size("xy")
    gz_index = lax.axis_index("gz")
    dev_index = lax.axis_index("dev")
    xy_index = lax.axis_index("xy")
    size_y, size_z, size_x = permittivity.shape
    keep_y = rim_keep_mask(size_y + 1, dev_index)
    keep_z = rim_keep_mask(size_z + 1, gz_index)
    keep_x = rim_keep_mask(size_x + 1, xy_index)
    rim_keep = keep_y[:, None, None] * keep_z[None, :, None] * keep_x[None, None, :]
    step_rate = COURANT / permittivity
    field_state = fields
    spectra_now = spectra
    for step_number in range(STEPS):
        electric, magnetic = yee_step(field_state, step_rate, rim_keep)
        field_state = jnp.concatenate([electric, magnetic])
        spectra_now = spectral_update(spectra_now, electric, magnetic, phase_start, step_number)
    grid_x = size_x * xy_count
    grid_y = size_y * dev_count
    grid_z = size_z * slab_count
    x_local = jnp.where(xy_index == 0, XB, size_x - 1 - XB).astype(jnp.int32)
    facing_x = jnp.where(xy_index == 0, -1.0, 1.0)
    wall_plane = lax.dynamic_slice_in_dim(spectra_now, x_local, 1, axis=3)[:, :, :, 0]
    wall_count = size_y * size_z // PATCH
    wall_records = (
        face_values(wall_plane, facing_x, X_PICKS).transpose(1, 0, 2).reshape(wall_count, 8 * PATCH)
    )
    z_local = jnp.where(gz_index == 0, ZB, size_z - 1 - ZB).astype(jnp.int32)
    facing_z = jnp.where(gz_index == 0, -1.0, 1.0)
    cap_plane = lax.dynamic_slice_in_dim(spectra_now, z_local, 1, axis=2)[:, :, 0, :]
    cap_count = size_y * size_x // PATCH
    cap_records = (
        face_values(cap_plane, facing_z, Z_PICKS)
        .reshape(8, cap_count, PATCH)
        .transpose(1, 0, 2)
        .reshape(cap_count, 8 * PATCH)
    )
    is_end = jnp.logical_or(gz_index == 0, gz_index == slab_count - 1)
    end_weight = jnp.where(is_end, 1.0, 0.0)
    wall_flat = jnp.arange(wall_count, dtype=jnp.int32) * PATCH
    wall_ones = jnp.ones((wall_count,), jnp.float32)
    wall_meta = jnp.stack(
        [
            wall_ones * (xy_index * size_x + x_local).astype(jnp.float32),
            (dev_index * size_y + wall_flat // size_z).astype(jnp.float32),
            (gz_index * size_z + wall_flat % size_z).astype(jnp.float32),
            wall_ones * jnp.where(xy_index == 0, 1.0, 2.0),
        ],
        axis=1,
    )
    owners = wall_owner[0]
    record_order = jnp.arange(wall_count, dtype=jnp.int32)
    earlier_same = (owners[:, None] == owners[None, :]) & (
        record_order[None, :] < record_order[:, None]
    )
    slot_rank = jnp.sum(earlier_same.astype(jnp.int32), axis=1)
    cap_share = cap_count // slab_count
    wall_most = (wall_count + slab_count - 1) // slab_count
    slot_index = owners * wall_most + slot_rank
    slot_range = jnp.arange(slab_count * wall_most, dtype=jnp.int32)
    send_onehot = jnp.where(slot_range[:, None] == slot_index[None, :], 1.0, 0.0).astype(
        jnp.float32
    )
    send_records = jnp.dot(send_onehot, wall_records, precision=HIGHEST).reshape(
        slab_count, wall_most, 8 * PATCH
    )
    send_meta = jnp.dot(send_onehot, wall_meta, precision=HIGHEST).reshape(slab_count, wall_most, 4)
    got_records, got_meta = (
        lax.all_to_all(send_records, "gz", split_axis=0, concat_axis=0, tiled=True),
        lax.all_to_all(send_meta, "gz", split_axis=0, concat_axis=0, tiled=True),
    )
    flat_records = got_records.reshape(slab_count * wall_most, 8 * PATCH)
    flat_meta = got_meta.reshape(slab_count * wall_most, 4)
    alive_slots = flat_meta[:, 3] > 0.5
    position = jnp.cumsum(alive_slots.astype(jnp.int32)) - 1
    own_onehot = jnp.where(
        (jnp.arange(wall_count, dtype=jnp.int32)[:, None] == position[None, :])
        & alive_slots[None, :],
        1.0,
        0.0,
    ).astype(jnp.float32)
    owned_walls = jnp.dot(own_onehot, flat_records, precision=HIGHEST)
    owned_wall_meta = jnp.dot(own_onehot, flat_meta, precision=HIGHEST)
    lower_got = broadcast(cap_records, "gz", 0)
    upper_got = broadcast(cap_records, "gz", slab_count - 1)
    lower_onehot = mine_selector(cap_owner[0], gz_index, cap_share)
    upper_onehot = mine_selector(cap_owner[1], gz_index, cap_share)
    lower_meta = cap_layout(cap_count, size_x, size_y, xy_index, dev_index, float(ZB), 3.0)
    upper_meta = cap_layout(
        cap_count, size_x, size_y, xy_index, dev_index, float(grid_z - 1 - ZB), 4.0
    )
    owned_rows = jnp.concatenate(
        [
            owned_walls,
            jnp.dot(lower_onehot, lower_got, precision=HIGHEST),
            jnp.dot(upper_onehot, upper_got, precision=HIGHEST),
        ]
    )
    owned_meta = jnp.concatenate(
        [
            owned_wall_meta,
            jnp.dot(lower_onehot, lower_meta, precision=HIGHEST),
            jnp.dot(upper_onehot, upper_meta, precision=HIGHEST),
        ]
    )
    unit_vectors, theta_hat, phi_hat = direction_frames(dir_index)
    centers = ((grid_x - 1) / 2.0, (grid_y - 1) / 2.0, (grid_z - 1) / 2.0)
    surface_count = 2 * grid_y * grid_z + 2 * grid_y * grid_x
    norm_scale = 1.0 / math.sqrt(2.0 * surface_count)
    currents, positions, x_flag = point_layout(owned_rows, owned_meta, centers, norm_scale)
    direction_count = unit_vectors.shape[0]
    block_size = min(512, direction_count)
    partial_far = jnp.concatenate(
        [
            far_block(unit_vectors[block_start : block_start + block_size], currents, positions)
            for block_start in range(0, direction_count, block_size)
        ],
        axis=1,
    )
    joined_index = (gz_index * dev_count + dev_index) * xy_count + xy_index
    share_count = direction_count // (slab_count * dev_count * xy_count)
    first_dir = joined_index * share_count
    far_total = lax.psum(partial_far, ("gz", "dev", "xy"))
    intensity_all, slope_total = intensity_and_slope(
        far_total, theta_hat, phi_hat, target, aim_mask
    )
    intensity = lax.dynamic_slice_in_dim(intensity_all, first_dir, share_count, 0)
    gradient = adjoint_block(unit_vectors[0:block_size], slope_total[:, 0:block_size], positions)
    for block_start in range(block_size, direction_count, block_size):
        gradient = gradient + adjoint_block(
            unit_vectors[block_start : block_start + block_size],
            slope_total[:, block_start : block_start + block_size],
            positions,
        )
    point_count = gradient.shape[1] // PATCH
    adjoint_records = (
        to_record(gradient * norm_scale, x_flag)
        .reshape(8, point_count, PATCH)
        .transpose(1, 0, 2)
        .reshape(point_count, 8 * PATCH)
    )
    spread_back = jnp.dot(own_onehot.T, adjoint_records[:wall_count], precision=HIGHEST).reshape(
        slab_count, wall_most, 8 * PATCH
    )
    returned = lax.all_to_all(spread_back, "gz", split_axis=0, concat_axis=0, tiled=True)
    wall_adjoint = jnp.dot(
        send_onehot.T, returned.reshape(slab_count * wall_most, 8 * PATCH), precision=HIGHEST
    )
    lower_part = adjoint_records[wall_count : wall_count + cap_share]
    upper_part = adjoint_records[wall_count + cap_share :]
    cap_sheet = jnp.stack(
        [
            jnp.dot(lower_onehot.T, lower_part, precision=HIGHEST),
            jnp.dot(upper_onehot.T, upper_part, precision=HIGHEST),
        ]
    )
    cap_sum = lax.psum(cap_sheet, "gz")
    cap_adjoint = jnp.where(gz_index == 0, cap_sum[0], cap_sum[1]) * end_weight
    adjoint_local = jnp.concatenate([wall_adjoint, cap_adjoint])
    return (
        field_state,
        spectra_now,
        owned_rows[None, None, None],
        intensity,
        adjoint_local[None, None, None],
    )


def solution(mesh):
    placed = (
        P("groups", "dev", "gz", "xy"),
        P("groups", "dev", "gz", "xy"),
        P(("groups", "dev"), "gz", "xy"),
        P("groups"),
        P("gz", None),
        P(),
        P(),
        P("groups"),
        P("groups"),
    )
    return jax.shard_map(
        local,
        mesh=mesh,
        in_specs=placed,
        out_specs=(
            P("groups", "dev", "gz", "xy"),
            P("groups", "dev", "gz", "xy"),
            P(("groups", "gz"), "dev", "xy", None, None),
            P(("groups", "gz", "dev", "xy")),
            P(("groups", "gz"), "dev", "xy", None, None),
        ),
        check_vma=False,
    )
```

profile of v0, /device:TPU:0, one launch (start us, length us, event | category | flops | bytes accessed | tf_op | source)
XLA Modules:
  0.0 339.4 jit_solution(17645889408166721853)
XLA Ops:
  8.9 6.3 %all-to-all-start = ((f32[4,1,4]{2,1,0:T(1,128)}), f32[4,1,4]{2,1,0:T(1,128)S(1)}, u32[]{:S(2)}, u32[]{:S(2)}) async-start(f32[4,1,4]{2,1,0:T(1,128)} %bitcast.46), calls=%async_computation | async-start | bytes 4096 | tf_op jit(solution)/shard_map/all_to_all | solution.py:330
  16.2 3.9 %collective-permute-start = (f32[6,4,1,128]{3,2,1,0:T(1,128)S(1)}, f32[6,4,1,128]{3,2,1,0:T(1,128)S(1)}, u32[]{:S(2)}, u32[]{:S(2)}) collective-permute-start(f32[6,4,1,128]{3,2,1,0:T(1,128)S(1)} %get-tuple-element.119), channel_id=1, source_target_pairs={{0,4},{4,8},{8,12},{1,5},{5,9},{9,13},{2,6},{6,10},{10,14},{3,7},{... | collective-permute-start | bytes 36872 | tf_op jit(solution)/shard_map/ppermute | solution.py:31
  20.2 1.3 collective-permute-start.1
  25.9 3.4 %collective-permute-start.2 = (f32[6,1,18,128]{3,2,1,0:T(8,128)S(1)}, f32[6,1,18,128]{3,2,1,0:T(8,128)S(1)}, u32[]{:S(2)}, u32[]{:S(2)}) collective-permute-start(f32[6,1,18,128]{3,2,1,0:T(8,128)S(1)} %get-tuple-element.113), channel_id=1, source_target_pairs={{0,2},{1,3},{4,6},{5,7},{8,10},{9,11},{12,14},{13,15},{16,18},{17,... | collective-permute-start | bytes 165896 | tf_op jit(solution)/shard_map/ppermute | solution.py:31
  29.3 1.3 collective-permute-start.3
  31.3 4.3 %collective-permute-done.3 = f32[6,1,18,128]{3,2,1,0:T(8,128)S(1)} collective-permute-done((f32[6,1,18,128]{3,2,1,0:T(8,128)S(1)}, f32[6,1,18,128]{3,2,1,0:T(8,128)S(1)}, u32[]{:S(2)}, u32[]{:S(2)}) %collective-permute-start.3) | collective-permute-done | bytes 55328 | tf_op jit(solution)/shard_map/ppermute | solution.py:32
  35.8 1.3 collective-permute-start.4
  37.2 1.3 collective-permute-start.5
  38.9 2.0 collective-permute-done.5
  42.3 4.5 %collective-permute-start.6 = (f32[6,4,1,128]{3,2,1,0:T(1,128)S(1)}, f32[6,4,1,128]{3,2,1,0:T(1,128)S(1)}, u32[]{:S(2)}, u32[]{:S(2)}) collective-permute-start(f32[6,4,1,128]{3,2,1,0:T(1,128)S(1)} %get-tuple-element.117), channel_id=1, source_target_pairs={{0,4},{4,8},{8,12},{1,5},{5,9},{9,13},{2,6},{6,10},{10,14},{3,7},{... | collective-permute-start | bytes 36872 | tf_op jit(solution)/shard_map/ppermute | solution.py:31
  46.9 1.3 collective-permute-start.7
  48.7 3.8 %collective-permute-done.7 = f32[6,4,1,128]{3,2,1,0:T(1,128)S(1)} collective-permute-done((f32[6,4,1,128]{3,2,1,0:T(1,128)S(1)}, f32[6,4,1,128]{3,2,1,0:T(1,128)S(1)}, u32[]{:S(2)}, u32[]{:S(2)}) %collective-permute-start.7) | collective-permute-done | bytes 12320 | tf_op jit(solution)/shard_map/ppermute | solution.py:32
  52.5 1.6 collective-permute-start.8
  54.1 1.3 collective-permute-start.9
  56.0 4.3 %collective-permute-done.9 = f32[6,1,18,128]{3,2,1,0:T(8,128)S(1)} collective-permute-done((f32[6,1,18,128]{3,2,1,0:T(8,128)S(1)}, f32[6,1,18,128]{3,2,1,0:T(8,128)S(1)}, u32[]{:S(2)}, u32[]{:S(2)}) %collective-permute-start.9) | collective-permute-done | bytes 55328 | tf_op jit(solution)/shard_map/ppermute | solution.py:32
  60.6 1.3 collective-permute-start.10
  62.0 1.3 collective-permute-start.11
  63.7 2.0 collective-permute-done.11
  66.4 3.4 collective-permute-start.12
  69.8 1.3 collective-permute-start.13
  71.2 4.2 %collective-permute-done.13 = f32[6,4,1,128]{3,2,1,0:T(1,128)S(1)} collective-permute-done((f32[6,4,1,128]{3,2,1,0:T(1,128)S(1)}, f32[6,4,1,128]{3,2,1,0:T(1,128)S(1)}, u32[]{:S(2)}, u32[]{:S(2)}) %collective-permute-start.13) | collective-permute-done | bytes 12320 | tf_op jit(solution)/shard_map/ppermute | solution.py:32
  75.4 1.6 collective-permute-start.14
  77.0 1.3 collective-permute-start.15
  79.0 4.3 %collective-permute-done.15 = f32[6,1,18,128]{3,2,1,0:T(8,128)S(1)} collective-permute-done((f32[6,1,18,128]{3,2,1,0:T(8,128)S(1)}, f32[6,1,18,128]{3,2,1,0:T(8,128)S(1)}, u32[]{:S(2)}, u32[]{:S(2)}) %collective-permute-start.15) | collective-permute-done | bytes 55328 | tf_op jit(solution)/shard_map/ppermute | solution.py:32
  83.5 1.3 collective-permute-start.16
  86.6 2.0 collective-permute-done.17
  92.1 3.2 all-to-all-start.1
  95.7 21.5 %all-reduce = (f32[32,128]{0,1:T(8,128)S(1)}, f32[32,128]{0,1:T(8,128)S(1)}) all-reduce(f32[32,128]{0,1:T(8,128)S(1)} %bitcast.259, f32[32,128]{0,1:T(8,128)S(1)} %bitcast.258), channel_id=1, replica_groups=mesh['groups'=2,'gz'=4,'dev'=2,'xy'=2] {'gz'}, use_global_device_ids=true, to_apply=%region_5.6 | all-reduce | flops 8192 | bytes 65536 | tf_op jit(solution)/shard_map/psum | solution.py:39
  119.0 2.8 fusion.40
  121.8 2.8 fusion.32
  124.6 2.8 fusion.26
  127.4 2.8 fusion.18
  130.2 3.2 fusion.12
  133.4 2.8 fusion.4
  136.3 2.8 fusion.46
  139.1 2.8 fusion.54
  141.9 3.0 convolution_add_fusion.3
  144.8 2.8 convolution_subtract_fusion.2
  147.7 2.8 convolution_add_fusion.2
  150.5 2.8 convolution_subtract_fusion.1
  153.3 3.0 convolution_add_fusion.1
  156.3 2.8 convolution_subtract_fusion
  159.1 2.8 convolution_add_fusion
  161.9 2.8 convolution_subtract_fusion.3
  166.2 85.2 %all-reduce.3.cloned.1.call-done = f32[12,2048]{1,0:T(8,128)} async-done(((f32[12,2048]{1,0:T(8,128)}), f32[12,2048]{1,0:T(8,128)}) %all-reduce.3.cloned.1.call-update) | async-done | bytes 98320 | tf_op jit(solution)/shard_map/psum | solution.py:383
  251.4 1.3 multiply_reduce_fusion.6
  253.6 3.3 fusion.21
  256.9 3.0 fusion.49
  259.9 3.0 fusion.35
  263.0 2.9 fusion.51
  265.9 3.0 fusion.37
  268.9 3.2 fusion.23
  272.2 3.0 convolution_subtract_fusion.5
  275.1 3.0 convolution_subtract_fusion.7
  278.1 3.0 convolution_subtract_fusion.6
  281.2 3.2 convolution_add_fusion.7
  284.4 3.0 convolution_add_fusion.6
  287.4 3.0 convolution_add_fusion.5
  290.4 3.0 fusion.7
  293.4 3.2 fusion.9
  296.6 3.0 convolution_subtract_fusion.4
  299.6 3.0 convolution_add_fusion.4
  304.5 6.1 %all-to-all-start.2 = ((f32[4,1,128]{2,1,0:T(1,128)}), f32[4,1,128]{2,1,0:T(1,128)S(1)}, u32[]{:S(2)}, u32[]{:S(2)}) async-start(f32[4,1,128]{2,1,0:T(1,128)} %bitcast.77), calls=%async_computation.2 | async-start | bytes 4096 | tf_op jit(solution)/shard_map/all_to_all | solution.py:405
  311.2 19.5 %psum.31 = f32[2,32,128]{2,1,0:T(8,128)S(1)} all-reduce(f32[2,32,128]{2,1,0:T(8,128)S(1)} %pad_maximum_fusion.34), channel_id=1, replica_groups=mesh['groups'=2,'gz'=4,'dev'=2,'xy'=2] {'gz'}, use_global_device_ids=true, to_apply=%region_15.16 | all-reduce | flops 8192 | bytes 65536 | tf_op jit(solution)/shard_map/psum | solution.py:417
  (229 shorter events, 25.1 us)
Async XLA Ops:
  7.3 0.7 copy-start.9
  8.9 16.6 %all-to-all-start = ((f32[4,1,4]{2,1,0:T(1,128)}), f32[4,1,4]{2,1,0:T(1,128)S(1)}, u32[]{:S(2)}, u32[]{:S(2)}) async-start(f32[4,1,4]{2,1,0:T(1,128)} %bitcast.46), calls=%async_computation | async-start | bytes 4096 | tf_op jit(solution)/shard_map/all_to_all | solution.py:330
  16.2 9.6 %collective-permute-start = (f32[6,4,1,128]{3,2,1,0:T(1,128)S(1)}, f32[6,4,1,128]{3,2,1,0:T(1,128)S(1)}, u32[]{:S(2)}, u32[]{:S(2)}) collective-permute-start(f32[6,4,1,128]{3,2,1,0:T(1,128)S(1)} %get-tuple-element.119), channel_id=1, source_target_pairs={{0,4},{4,8},{8,12},{1,5},{5,9},{9,13},{2,6},{6,10},{10,14},{3,7},{... | collective-permute-start | bytes 36872 | tf_op jit(solution)/shard_map/ppermute | solution.py:31
  20.2 5.7 %collective-permute-start.1 = (f32[6,4,1,128]{3,2,1,0:T(1,128)S(1)}, f32[6,4,1,128]{3,2,1,0:T(1,128)S(1)}, u32[]{:S(2)}, u32[]{:S(2)}) collective-permute-start(f32[6,4,1,128]{3,2,1,0:T(1,128)S(1)} %get-tuple-element.120), channel_id=1, source_target_pairs={{4,0},{8,4},{12,8},{5,1},{9,5},{13,9},{6,2},{10,6},{14,10},{7,3},{... | collective-permute-start | bytes 36872 | tf_op jit(solution)/shard_map/ppermute | solution.py:32
  23.3 0.7 copy-start.8
  24.2 0.7 copy-start.4
  24.3 1.6 copy-start
  25.9 5.4 %collective-permute-start.2 = (f32[6,1,18,128]{3,2,1,0:T(8,128)S(1)}, f32[6,1,18,128]{3,2,1,0:T(8,128)S(1)}, u32[]{:S(2)}, u32[]{:S(2)}) collective-permute-start(f32[6,1,18,128]{3,2,1,0:T(8,128)S(1)} %get-tuple-element.113), channel_id=1, source_target_pairs={{0,2},{1,3},{4,6},{5,7},{8,10},{9,11},{12,14},{13,15},{16,18},{17,... | collective-permute-start | bytes 165896 | tf_op jit(solution)/shard_map/ppermute | solution.py:31
  29.3 6.2 %collective-permute-start.3 = (f32[6,1,18,128]{3,2,1,0:T(8,128)S(1)}, f32[6,1,18,128]{3,2,1,0:T(8,128)S(1)}, u32[]{:S(2)}, u32[]{:S(2)}) collective-permute-start(f32[6,1,18,128]{3,2,1,0:T(8,128)S(1)} %get-tuple-element.114), channel_id=1, source_target_pairs={{2,0},{3,1},{6,4},{7,5},{10,8},{11,9},{14,12},{15,13},{18,16},{19,... | collective-permute-start | bytes 165896 | tf_op jit(solution)/shard_map/ppermute | solution.py:32
  35.8 2.7 collective-permute-start.4
  37.2 3.7 %collective-permute-start.5 = (f32[6,6,18,1]{3,2,1,0:T(8,128)S(1)}, f32[6,6,18,1]{3,2,1,0:T(8,128)S(1)}, u32[]{:S(2)}, u32[]{:S(2)}) collective-permute-start(f32[6,6,18,1]{3,2,1,0:T(8,128)S(1)} %get-tuple-element.108), channel_id=1, source_target_pairs={{1,0},{3,2},{5,4},{7,6},{9,8},{11,10},{13,12},{15,14},{17,16},{19,... | collective-permute-start | bytes 7784 | tf_op jit(solution)/shard_map/ppermute | solution.py:32
  41.0 0.8 copy-start.1
  42.3 6.3 %collective-permute-start.6 = (f32[6,4,1,128]{3,2,1,0:T(1,128)S(1)}, f32[6,4,1,128]{3,2,1,0:T(1,128)S(1)}, u32[]{:S(2)}, u32[]{:S(2)}) collective-permute-start(f32[6,4,1,128]{3,2,1,0:T(1,128)S(1)} %get-tuple-element.117), channel_id=1, source_target_pairs={{0,4},{4,8},{8,12},{1,5},{5,9},{9,13},{2,6},{6,10},{10,14},{3,7},{... | collective-permute-start | bytes 36872 | tf_op jit(solution)/shard_map/ppermute | solution.py:31
  46.9 5.6 %collective-permute-start.7 = (f32[6,4,1,128]{3,2,1,0:T(1,128)S(1)}, f32[6,4,1,128]{3,2,1,0:T(1,128)S(1)}, u32[]{:S(2)}, u32[]{:S(2)}) collective-permute-start(f32[6,4,1,128]{3,2,1,0:T(1,128)S(1)} %get-tuple-element.118), channel_id=1, source_target_pairs={{4,0},{8,4},{12,8},{5,1},{9,5},{13,9},{6,2},{10,6},{14,10},{7,3},{... | collective-permute-start | bytes 36872 | tf_op jit(solution)/shard_map/ppermute | solution.py:32
  52.5 3.5 %collective-permute-start.8 = (f32[6,1,18,128]{3,2,1,0:T(8,128)S(1)}, f32[6,1,18,128]{3,2,1,0:T(8,128)S(1)}, u32[]{:S(2)}, u32[]{:S(2)}) collective-permute-start(f32[6,1,18,128]{3,2,1,0:T(8,128)S(1)} %get-tuple-element.111), channel_id=1, source_target_pairs={{0,2},{1,3},{4,6},{5,7},{8,10},{9,11},{12,14},{13,15},{16,18},{17,... | collective-permute-start | bytes 165896 | tf_op jit(solution)/shard_map/ppermute | solution.py:31
  54.1 6.2 %collective-permute-start.9 = (f32[6,1,18,128]{3,2,1,0:T(8,128)S(1)}, f32[6,1,18,128]{3,2,1,0:T(8,128)S(1)}, u32[]{:S(2)}, u32[]{:S(2)}) collective-permute-start(f32[6,1,18,128]{3,2,1,0:T(8,128)S(1)} %get-tuple-element.112), channel_id=1, source_target_pairs={{2,0},{3,1},{6,4},{7,5},{10,8},{11,9},{14,12},{15,13},{18,16},{19,... | collective-permute-start | bytes 165896 | tf_op jit(solution)/shard_map/ppermute | solution.py:32
  60.6 2.7 collective-permute-start.10
  62.0 3.7 %collective-permute-start.11 = (f32[6,6,18,1]{3,2,1,0:T(8,128)S(1)}, f32[6,6,18,1]{3,2,1,0:T(8,128)S(1)}, u32[]{:S(2)}, u32[]{:S(2)}) collective-permute-start(f32[6,6,18,1]{3,2,1,0:T(8,128)S(1)} %get-tuple-element.106), channel_id=1, source_target_pairs={{1,0},{3,2},{5,4},{7,6},{9,8},{11,10},{13,12},{15,14},{17,16},{19,... | collective-permute-start | bytes 7784 | tf_op jit(solution)/shard_map/ppermute | solution.py:32
  66.4 4.8 %collective-permute-start.12 = (f32[6,4,1,128]{3,2,1,0:T(1,128)S(1)}, f32[6,4,1,128]{3,2,1,0:T(1,128)S(1)}, u32[]{:S(2)}, u32[]{:S(2)}) collective-permute-start(f32[6,4,1,128]{3,2,1,0:T(1,128)S(1)} %get-tuple-element.115), channel_id=1, source_target_pairs={{0,4},{4,8},{8,12},{1,5},{5,9},{9,13},{2,6},{6,10},{10,14},{3,7},{... | collective-permute-start | bytes 36872 | tf_op jit(solution)/shard_map/ppermute | solution.py:31
  69.8 5.6 %collective-permute-start.13 = (f32[6,4,1,128]{3,2,1,0:T(1,128)S(1)}, f32[6,4,1,128]{3,2,1,0:T(1,128)S(1)}, u32[]{:S(2)}, u32[]{:S(2)}) collective-permute-start(f32[6,4,1,128]{3,2,1,0:T(1,128)S(1)} %get-tuple-element.116), channel_id=1, source_target_pairs={{4,0},{8,4},{12,8},{5,1},{9,5},{13,9},{6,2},{10,6},{14,10},{7,3},{... | collective-permute-start | bytes 36872 | tf_op jit(solution)/shard_map/ppermute | solution.py:32
  75.4 3.5 %collective-permute-start.14 = (f32[6,1,18,128]{3,2,1,0:T(8,128)S(1)}, f32[6,1,18,128]{3,2,1,0:T(8,128)S(1)}, u32[]{:S(2)}, u32[]{:S(2)}) collective-permute-start(f32[6,1,18,128]{3,2,1,0:T(8,128)S(1)} %get-tuple-element.109), channel_id=1, source_target_pairs={{0,2},{1,3},{4,6},{5,7},{8,10},{9,11},{12,14},{13,15},{16,18},{17,... | collective-permute-start | bytes 165896 | tf_op jit(solution)/shard_map/ppermute | solution.py:31
  77.0 6.2 %collective-permute-start.15 = (f32[6,1,18,128]{3,2,1,0:T(8,128)S(1)}, f32[6,1,18,128]{3,2,1,0:T(8,128)S(1)}, u32[]{:S(2)}, u32[]{:S(2)}) collective-permute-start(f32[6,1,18,128]{3,2,1,0:T(8,128)S(1)} %get-tuple-element.110), channel_id=1, source_target_pairs={{2,0},{3,1},{6,4},{7,5},{10,8},{11,9},{14,12},{15,13},{18,16},{19,... | collective-permute-start | bytes 165896 | tf_op jit(solution)/shard_map/ppermute | solution.py:32
  83.5 2.7 collective-permute-start.16
  84.9 3.7 %collective-permute-start.17 = (f32[6,6,18,1]{3,2,1,0:T(8,128)S(1)}, f32[6,6,18,1]{3,2,1,0:T(8,128)S(1)}, u32[]{:S(2)}, u32[]{:S(2)}) collective-permute-start(f32[6,6,18,1]{3,2,1,0:T(8,128)S(1)} %get-tuple-element.104), channel_id=1, source_target_pairs={{1,0},{3,2},{5,4},{7,6},{9,8},{11,10},{13,12},{15,14},{17,16},{19,... | collective-permute-start | bytes 7784 | tf_op jit(solution)/shard_map/ppermute | solution.py:32
  88.9 1.0 copy-start.3
  90.1 5.3 %copy-start.2 = (f32[12,4,16,128]{3,2,1,0:T(8,128)}, f32[12,4,16,128]{3,2,1,0:T(8,128)S(1)}, u32[]{:S(2)}) copy-start(f32[12,4,16,128]{3,2,1,0:T(8,128)S(1)} %pad_maximum_fusion.3) | copy-start | bytes 1179652
  92.1 25.7 %all-to-all-start.1 = ((f32[4,1,128]{2,1,0:T(1,128)}), f32[4,1,128]{2,1,0:T(1,128)S(1)}, u32[]{:S(2)}, u32[]{:S(2)}) async-start(f32[4,1,128]{2,1,0:T(1,128)} %bitcast.50), calls=%async_computation.1 | async-start | bytes 4096 | tf_op jit(solution)/shard_map/all_to_all | solution.py:329
  95.3 156.1 %all-reduce.3.cloned.1.call-start = ((), (), s32[]{:S(2)}) async-start(), calls=%async_computation.3 | async-start | bytes 262144 | tf_op jit(solution)/shard_map/psum | solution.py:383
  165.5 87.9 %copy-start.7 = (f32[6,4,16,128]{3,2,1,0:T(8,128)}, f32[6,4,16,128]{3,2,1,0:T(8,128)S(1)}, u32[]{:S(2)}) copy-start(f32[6,4,16,128]{3,2,1,0:T(8,128)S(1)} %constant_dynamic-update-slice_fusion.12) | copy-start | bytes 589828
  251.4 1.3 copy-start.6
  252.7 0.7 copy-start.5
  304.5 26.8 %all-to-all-start.2 = ((f32[4,1,128]{2,1,0:T(1,128)}), f32[4,1,128]{2,1,0:T(1,128)S(1)}, u32[]{:S(2)}, u32[]{:S(2)}) async-start(f32[4,1,128]{2,1,0:T(1,128)} %bitcast.77), calls=%async_computation.2 | async-start | bytes 4096 | tf_op jit(solution)/shard_map/all_to_all | solution.py:405
Sparse Core Ops, SparseCore 0:
  165.6 85.7 all-reduce.2
where the time goes:
time: 346 us; the launch traced here: 339 us
  waiting for transfers between devices  114 us (33%)
  matrix products  98.6 us (28%)
  starting transfers between devices  49.7 us (14%)
  blocking collectives  41 us (12%)
  between operations  17 us (5%)
  local copies, waits for them, and re-layouts  12.6 us (4%)
  other arithmetic  6.95 us (2%)
    psum x1, waiting for transfers between devices, local(): far_total = lax.psum(partial_far, ('gz', 'dev', 'xy'))  85.2 us
    ppermute x9, waiting for transfers between devices, padded_2(): after = lax.ppermute(first, axis, down)  26.8 us
    ppermute x9, starting transfers between devices, padded_2(): before = lax.ppermute(last, axis, up)  22.3 us
    psum x1, blocking collectives, broadcast(): return lax.psum(block, axis)  21.5 us
    psum x1, blocking collectives, local(): cap_sum = lax.psum(cap_sheet, 'gz')  19.5 us
    dot_general x4, matrix products, adjoint_block(): jnp.dot(slope_block[:6], cosine_table.T, precision=HIGHEST)  12.3 us
    dot_general x4, matrix products, adjoint_block(): jnp.dot(slope_block[6:], cosine_table.T, precision=HIGHEST)  12.3 us
    dot_general x4, matrix products, adjoint_block(): jnp.dot(slope_block[6:], sine_table.T, precision=HIGHEST)  12.3 us
  transfers between devices with their start and end apart: 22, of which 12 were waited for; matrix products, arithmetic and copies ran while one was open for 2% of the time, Pallas kernels for 0%

commit v1 on v0

v1 whole, which is shorter than its diff:
```python
import functools
import math

import jax
import jax.numpy as jnp
from jax import lax
from jax.experimental import pallas as pl
from jax.experimental.pallas import tpu as pltpu
from jax.sharding import PartitionSpec as P

PATCH = 16
XB = 8
ZB = 4
STEPS = 3
THETAS = 64
COURANT = 0.5
ANGULAR_STEP = 0.3
WAVE_NUMBER = 0.6
LANES = 128
HIGHEST = lax.Precision.HIGHEST
CURRENT_SIGNS = (-1.0, 1.0, 1.0, -1.0)
X_PICKS = (5, 4, 2, 1)
Z_PICKS = (4, 3, 1, 0)
MESH = pl.DeviceIdType.MESH
AXES = ("dev", "gz", "xy")
F32 = jnp.float32
BF16 = jnp.bfloat16


def iota(shape, dim):
    return lax.broadcasted_iota(jnp.int32, shape, dim)


def sincos(turns):
    half = (turns - jnp.floor(turns + 0.5)) * math.pi
    sq = half * half
    sin_h = half * (1.0 + sq * (-1.0 / 6 + sq * (1.0 / 120 + sq * (-1.0 / 5040 + sq * (1.0 / 362880 - sq * (1.0 / 39916800))))))
    cos_h = 1.0 + sq * (-0.5 + sq * (1.0 / 24 + sq * (-1.0 / 720 + sq * (1.0 / 40320 + sq * (-1.0 / 3628800 + sq * (1.0 / 479001600))))))
    return 2.0 * sin_h * cos_h, 1.0 - 2.0 * sin_h * sin_h


def split(values):
    high = values.astype(BF16)
    return high, (values - high.astype(F32)).astype(BF16)


def block_transpose(tile):
    on_diagonal = (iota(tile.shape, 1) // PATCH) == iota(tile.shape, 0)
    total = jnp.where(on_diagonal, tile, 0.0)
    for k in range(1, 8):
        turned = pltpu.roll(tile, PATCH * k, 1)
        total = total + pltpu.roll(jnp.where(on_diagonal, turned, 0.0), 8 - k, 0)
    return total


def kernel(
    sizes,
    fields, spectra, permit, phase, wall_owner, cap_owner, dirs, target, aim,
    fields_out, spectra_out, owned_out, intensity_out, adjoint_out,
    send_y, send_z, send_x, got_y, got_z, got_x,
    geo, weights, phases, table_hi, table_lo, cap_plane, lhs,
    parts_out, parts_in, slopes, walls, caps,
    halo_send, halo_got, part_send, part_got, slope_send, slope_got, wall_send, wall_got, cap_send, cap_got,
):
    slabs, devs, xys = sizes
    peers = slabs * devs * xys
    size_y, size_z, size_x = permit.shape
    chunks = dirs.shape[0]
    ratio = peers // chunks
    groups = 2 * size_y
    half_rows = 8 * size_y
    all_rows = 2 * half_rows
    gz, dev, xy = lax.axis_index("gz"), lax.axis_index("dev"), lax.axis_index("xy")
    me = (gz * devs + dev) * xys + xy
    place = {"dev": dev, "gz": gz, "xy": xy}
    count = {"dev": devs, "gz": slabs, "xy": xys}

    def ident(flat):
        return {"gz": flat // (devs * xys), "dev": (flat // xys) % devs, "xy": flat % xys}

    barrier = pltpu.get_barrier_semaphore()

    def greet(k, carry):
        pl.semaphore_signal(barrier, inc=1, device_id=ident((me + k) % peers), device_id_type=MESH)
        return carry

    lax.fori_loop(1, peers, greet, 0)

    index = dirs[...]
    sin_t, cos_t = sincos(((index // THETAS).astype(F32) + 0.5) * (0.5 / THETAS))
    sin_f, cos_f = sincos((index % THETAS).astype(F32) * (1.0 / THETAS))
    wave = WAVE_NUMBER / (2.0 * math.pi)
    for slot, values in enumerate((
        wave * sin_t * cos_f, wave * sin_t * sin_f, wave * cos_t,
        cos_t * cos_f, cos_t * sin_f, -sin_t, -sin_f, cos_f,
    )):
        geo[slot] = values

    grid_x, grid_y, grid_z = size_x * xys, size_y * devs, size_z * slabs
    x_first = (xy * size_x).astype(F32) - (grid_x - 1) / 2.0
    y_first = (dev * size_y).astype(F32) - (grid_y - 1) / 2.0
    z_first = (gz * size_z).astype(F32) - (grid_z - 1) / 2.0
    x_wall = jnp.where(xy == 0, XB, size_x - 1 - XB)
    z_cap = jnp.where(gz == 0, ZB, size_z - 1 - ZB)
    x_face = x_first + x_wall.astype(F32)
    z_face = z_first + z_cap.astype(F32)
    facing_x = jnp.where(xy == 0, -1.0, 1.0)
    facing_z = jnp.where(gz == 0, -1.0, 1.0)
    is_end = jnp.logical_or(gz == 0, gz == slabs - 1)
    end_weight = jnp.where(is_end, 1.0, 0.0)
    norm = 1.0 / math.sqrt(2.0 * (2 * grid_y * grid_z + 2 * grid_y * grid_x))

    def make_tables(j, carry):
        def row(slot):
            return geo[slot, pl.ds(j, 1), :]

        ux, uy, uz = row(0), row(1), row(2)
        blocks = size_x // 8
        far_s, far_c = sincos((iota((blocks, LANES), 0).astype(F32) * 8.0 + x_first) * ux)
        near_s, near_c = sincos(iota((8, LANES), 0).astype(F32) * ux)
        far_s, far_c = far_s[:, None, :], far_c[:, None, :]
        near_s, near_c = near_s[None], near_c[None]
        cos_x = (far_c * near_c - far_s * near_s).reshape(size_x, LANES)
        sin_x = (far_s * near_c + far_c * near_s).reshape(size_x, LANES)
        sin_z, cos_z = sincos((iota((size_z, LANES), 0).astype(F32) + z_first) * uz)
        for at, (x_part, z_part) in enumerate(((cos_x, cos_z), (sin_x, sin_z))):
            lanes = pl.ds(at * LANES, LANES)
            x_high, x_low = split(x_part)
            z_high, z_low = split(z_part)
            table_hi[j, pl.ds(0, size_x), lanes] = x_high
            table_lo[j, pl.ds(0, size_x), lanes] = x_low
            table_hi[j, pl.ds(size_x, 8 * size_z), lanes] = jnp.concatenate([z_high] * 8, axis=0)
            table_lo[j, pl.ds(size_x, 8 * size_z), lanes] = jnp.concatenate([z_low] * 8, axis=0)
        which = iota((groups, LANES), 0)
        cell_y = (which % size_y).astype(F32) + y_first
        sin_g, cos_g = sincos(cell_y * uy + jnp.where(which < size_y, z_face * uz, x_face * ux))
        phases[j, 0] = cos_g
        phases[j, 1] = sin_g
        kind = iota((8, LANES), 0) % 4

        def pattern(a, b, c, d):
            return jnp.where(kind == 0, a, jnp.where(kind == 1, b, jnp.where(kind == 2, c, d)))

        tx, ty, tz, fx, fy = row(3), row(4), row(5), row(6), row(7)
        weights[j, 0] = pattern(-tx, -ty, -fx, -fy)
        weights[j, 1] = pattern(-fx, -fy, tx, ty)
        weights[j, 2] = pattern(-ty, -tz, -fy, jnp.zeros_like(fy))
        weights[j, 3] = pattern(-fy, jnp.zeros_like(fy), ty, tz)
        return carry

    windows = 2 * STEPS

    def tables_of(window):
        lax.fori_loop(window * chunks // windows, (window + 1) * chunks // windows, make_tables, 0)

    order = iota((8, LANES), 0).astype(F32)
    run_s, run_c = sincos((phase[0] + 0.5 * ANGULAR_STEP * (order + 1.0)) * (0.5 / math.pi))

    for number, (axis, got) in enumerate(zip(AXES, (got_y, got_z, got_x))):
        @pl.when(place[axis] == count[axis] - 1)
        def _():
            for window in range(0, windows, 2):
                got[window] = jnp.zeros(got.shape[1:], F32)

        @pl.when(place[axis] == 0)
        def _():
            for window in range(1, windows, 2):
                got[window] = jnp.zeros(got.shape[1:], F32)

    pl.semaphore_wait(barrier, peers - 1)

    lane = iota((size_z, LANES), 1)
    lane3 = iota((size_y, size_z, LANES), 2)
    row3 = iota((size_y, size_z, LANES), 1)

    def halo_copies(window):
        step = -1 if window % 2 == 0 else 1
        copies = []
        for number, (axis, source, landing) in enumerate(
            zip(AXES, (send_y, send_z, send_x), (got_y, got_z, got_x))
        ):
            mine, total = place[axis], count[axis]
            copy = pltpu.make_async_remote_copy(
                src_ref=source.at[window],
                dst_ref=landing.at[window],
                send_sem=halo_send.at[window, number],
                recv_sem=halo_got.at[window, number],
                device_id={axis: (mine + step + total) % total},
                device_id_type=MESH,
            )
            if step < 0:
                copies.append((copy, mine > 0, mine < total - 1))
            else:
                copies.append((copy, mine < total - 1, mine > 0))
        return copies

    def start_halo(window, for_y, for_z, for_x):
        ahead = window % 2 == 0
        at_y, at_z = (0, 0) if ahead else (size_y - 1, size_z - 1)
        for k in range(2):
            send_y[window, k] = for_y[k][at_y]
            send_z[window, k] = for_z[k][:, at_z : at_z + 1, :]
        packed = jnp.zeros((size_z, LANES), F32)
        for k in range(2):
            for y in range(size_y):
                spot = k * size_y + y
                amount = spot if ahead else (spot + 1) % LANES
                value = for_x[k][y]
                turned = pltpu.roll(value, amount, 1) if amount else value
                packed = jnp.where(lane == spot, turned, packed)
        send_x[window] = packed
        for copy, sends, receives in halo_copies(window):
            @pl.when(sends)
            def _():
                copy.start()

    def wait_halo(window):
        for copy, sends, receives in halo_copies(window):
            @pl.when(receives)
            def _():
                copy.wait_recv()

    def shift_y(window, k, value):
        other = got_y[window, k][None]
        if window % 2 == 0:
            return jnp.concatenate([value[1:], other], axis=0) - value
        return value - jnp.concatenate([other, value[:-1]], axis=0)

    def shift_z(window, k, value):
        other = got_z[window, k]
        if window % 2 == 0:
            return jnp.where(row3 == size_z - 1, other, pltpu.roll(value, size_z - 1, 1)) - value
        return value - jnp.where(row3 == 0, other, pltpu.roll(value, 1, 1))

    def shift_x(window, k, value):
        landed = got_x[window]
        edges = []
        for y in range(size_y):
            spot = k * size_y + y
            if window % 2 == 0:
                edges.append(pltpu.roll(landed, LANES - 1 - spot, 1))
            else:
                amount = (LANES - spot) % LANES
                edges.append(pltpu.roll(landed, amount, 1) if amount else landed)
        other = jnp.stack(edges, axis=0)
        if window % 2 == 0:
            return jnp.where(lane3 == size_x - 1, other, pltpu.roll(value, size_x - 1, 2)) - value
        return value - jnp.where(lane3 == 0, other, pltpu.roll(value, 1, 2))

    ex, ey, ez = fields[0], fields[1], fields[2]
    start_halo(0, (ez, ex), (ey, ex), (ez, ey))
    rate = COURANT / permit[...]
    hx, hy, hz = fields[3], fields[4], fields[5]
    spec_from = spectra
    for n in range(STEPS):
        window = 2 * n
        tables_of(window)
        wait_halo(window)
        hx = hx - COURANT * (shift_y(window, 0, ez) - shift_z(window, 0, ey))
        hy = hy - COURANT * (shift_z(window, 1, ex) - shift_x(window, 0, ez))
        hz = hz - COURANT * (shift_x(window, 1, ey) - shift_y(window, 1, ex))
        window = 2 * n + 1
        start_halo(window, (hz, hx), (hy, hx), (hz, hy))
        half_c, half_s = run_c[2 * n : 2 * n + 1, :], run_s[2 * n : 2 * n + 1, :]
        for c, value in enumerate((hx, hy, hz)):
            spectra_out[3 + c] = spec_from[3 + c] + value * half_c
            spectra_out[9 + c] = spec_from[9 + c] - value * half_s
        tables_of(window)
        wait_halo(window)
        ex = ex + rate * (shift_y(window, 0, hz) - shift_z(window, 0, hy))
        ey = ey + rate * (shift_z(window, 1, hx) - shift_x(window, 0, hz))
        ez = ez + rate * (shift_x(window, 1, hy) - shift_y(window, 1, hx))
        if n < STEPS - 1:
            start_halo(window + 1, (ez, ex), (ey, ex), (ez, ey))
        full_c, full_s = run_c[2 * n + 1 : 2 * n + 2, :], run_s[2 * n + 1 : 2 * n + 2, :]
        for c, value in enumerate((ex, ey, ez)):
            spectra_out[c] = spec_from[c] + value * full_c
            spectra_out[6 + c] = spec_from[6 + c] - value * full_s
        spec_from = spectra_out
    for c, value in enumerate((ex, ey, ez, hx, hy, hz)):
        fields_out[c] = value

    own_walls = walls.at[gz]
    lane_block = iota((8, LANES), 1) // PATCH
    sub = iota((8, LANES), 0)
    own_block = lane_block == sub
    z_row = iota((size_z, LANES), 0)
    own_walls[...] = jnp.zeros((8, LANES), F32)
    for y in range(size_y):
        spread = jnp.zeros((size_z, LANES), F32)
        for c in range(8):
            k = c % 4
            from_c = X_PICKS[k] + (6 if c >= 4 else 0)
            column = jnp.sum(jnp.where(lane == x_wall, spectra_out[from_c, y], 0.0), axis=1, keepdims=True)
            spread = jnp.where(lane == c * PATCH + z_row, column * (CURRENT_SIGNS[k] * facing_x), spread)
        record = jnp.sum(spread, axis=0, keepdims=True)
        own_walls[pl.ds(y, 1), :] = record
        for c in range(8):
            k = c % 4
            from_c = Z_PICKS[k] + (6 if c >= 4 else 0)
            low = spectra_out[from_c, y, pl.ds(ZB, 1), :]
            high = spectra_out[from_c, y, pl.ds(size_z - 1 - ZB, 1), :]
            picked = jnp.where(gz == 0, low, high) * (CURRENT_SIGNS[k] * facing_z * end_weight)
            cap_plane[pl.ds(8 * y + c, 1), :] = picked
        wall_hi, wall_lo = split(jnp.where(own_block, record, 0.0) * norm)
        cap_hi, cap_lo = split(cap_plane[pl.ds(8 * y, 8), :] * norm)
        none = jnp.zeros((8, LANES), BF16)
        for at, (cap_part, wall_part) in enumerate(((cap_hi, wall_hi), (cap_lo, wall_lo))):
            first = at * all_rows + 8 * y
            lhs[pl.ds(first, 8), :] = jnp.concatenate([cap_part, none], axis=1)
            lhs[pl.ds(first + half_rows, 8), :] = jnp.concatenate([none, wall_part], axis=1)

    sign = jnp.where(sub < 4, -1.0, 1.0)

    def far_of(j, carry):
        rows = lhs[...]
        by_high = jnp.dot(rows, table_hi[j], preferred_element_type=F32)
        by_low = jnp.dot(rows[:all_rows], table_lo[j], preferred_element_type=F32)
        product = by_high[:all_rows] + by_high[all_rows:] + by_low
        theta = jnp.zeros((8, LANES), F32)
        phi = jnp.zeros((8, LANES), F32)
        for face in range(2):
            sum_c = jnp.zeros((8, LANES), F32)
            sum_s = jnp.zeros((8, LANES), F32)
            for y in range(size_y):
                g = face * size_y + y
                tile = product[8 * g : 8 * g + 8]
                tile = tile[:, :LANES] + sign * pltpu.roll(tile[:, LANES:], 4, 0)
                sum_c = sum_c + tile * phases[j, 0, pl.ds(g, 1), :]
                sum_s = sum_s + tile * phases[j, 1, pl.ds(g, 1), :]
            far = sum_c + sign * pltpu.roll(sum_s, 4, 0)
            theta = theta + weights[j, 2 * face] * far
            phi = phi + weights[j, 2 * face + 1] * far

        def four(values):
            pairs = values + pltpu.roll(values, 7, 0)
            return pairs + pltpu.roll(pairs, 6, 0)

        parts_out[j] = jnp.where(sub % 4 == 1, pltpu.roll(four(phi), 1, 0), four(theta))
        return carry

    lax.fori_loop(0, chunks, far_of, 0)

    def part_copy(k):
        peer = (me + k) % peers
        return pltpu.make_async_remote_copy(
            src_ref=parts_out.at[peer // ratio],
            dst_ref=parts_in.at[k],
            send_sem=part_send.at[k],
            recv_sem=part_got.at[k],
            device_id=ident(peer),
            device_id_type=MESH,
        )

    def each_peer(act):
        def body(k, carry):
            act(k)
            return carry

        lax.fori_loop(1, peers, body, 0)

    each_peer(lambda k: part_copy(k).start())

    lanes8 = iota((1, LANES), 1)
    owner_row = jnp.zeros((1, LANES), F32)
    for p in range(size_y):
        owner_row = jnp.where(lanes8 == 8 * gz + p, (wall_owner[0, p] + 1).astype(F32), owner_row)
    own_walls[pl.ds(size_y, 1), :] = owner_row

    def wall_copy(k):
        return pltpu.make_async_remote_copy(
            src_ref=walls.at[gz],
            dst_ref=walls.at[gz],
            send_sem=wall_send.at[k],
            recv_sem=wall_got.at[gz],
            device_id={"gz": (gz + k) % slabs},
            device_id_type=MESH,
        )

    def wall_landing(s):
        return pltpu.make_async_remote_copy(
            src_ref=walls.at[s], dst_ref=walls.at[s], send_sem=wall_send.at[0], recv_sem=wall_got.at[s],
            device_id={"gz": (gz + 1) % slabs}, device_id_type=MESH,
        )

    def cap_copy(k, at):
        return pltpu.make_async_remote_copy(
            src_ref=caps.at[at],
            dst_ref=caps.at[at],
            send_sem=cap_send.at[k],
            recv_sem=cap_got.at[at],
            device_id={"gz": (gz + k) % slabs},
            device_id_type=MESH,
        )

    for k in range(1, slabs):
        wall_copy(k).start()
    for at, holder in enumerate((0, slabs - 1)):
        @pl.when(gz == holder)
        def _():
            for y in range(size_y):
                caps[at, pl.ds(8 * y, 8), :] = block_transpose(cap_plane[pl.ds(8 * y, 8), :])
            for k in range(1, slabs):
                cap_copy(k, at).start()

    parts_in[0] = parts_out[me // ratio]
    each_peer(lambda k: part_copy(k).wait_recv())
    field = jnp.sum(parts_in[...], axis=0)
    chunk = me // ratio
    power = jnp.where(sub % 4 < 2, field * field, 0.0)
    intensity = jnp.sum(power, axis=0, keepdims=True)
    intensity_out[...] = intensity
    residual = aim[pl.ds(chunk, 1), :].astype(F32) * (intensity - target[pl.ds(chunk, 1), :])
    leads = me % ratio == 0

    def slope_copy(k, of):
        return pltpu.make_async_remote_copy(
            src_ref=slopes.at[of],
            dst_ref=slopes.at[of],
            send_sem=slope_send.at[k],
            recv_sem=slope_got.at[of],
            device_id=ident((me + k) % peers),
            device_id_type=MESH,
        )

    @pl.when(leads)
    def _():
        slopes[chunk] = 2.0 * residual * field
        each_peer(lambda k: slope_copy(k, chunk).start())

    for s in range(slabs):
        @pl.when(s != gz)
        def _():
            wall_landing(s).wait_recv()
    for at, holder in enumerate((0, slabs - 1)):
        @pl.when(gz != holder)
        def _():
            cap_copy(1, at).wait_recv()

    def choose(mine, share, records):
        length = mine.shape[1]
        before = jnp.where(iota((length, length), 0) < iota((length, length), 1), 1.0, 0.0).astype(BF16)
        ones = jnp.broadcast_to(jnp.where(mine, 1.0, 0.0), (8, length))
        rank = jnp.dot(ones.astype(BF16), before, preferred_element_type=F32)
        wanted = iota((8, length), 0).astype(F32)
        chooser = jnp.where(rank == wanted, ones, 0.0)
        return jnp.dot(chooser, records, precision=HIGHEST, preferred_element_type=F32)[:share]

    all_walls = walls[...]
    owner_all = jnp.sum(all_walls[:, size_y : size_y + 1, :], axis=0)[:, : 8 * slabs]
    cap_share = (owned_out.shape[0] - size_y) // 2
    owned_out[pl.ds(0, size_y), :] = choose(
        owner_all == (gz + 1).astype(F32), size_y, all_walls.reshape(8 * slabs, LANES)
    )
    for at in range(2):
        owned_out[pl.ds(size_y + at * cap_share, cap_share), :] = choose(
            cap_owner[pl.ds(at, 1), :] == gz, cap_share, caps[at]
        )

    def await_slope(k):
        sender = (me + peers - k) % peers

        @pl.when(sender % ratio == 0)
        def _():
            slope_copy(1, sender // ratio).wait_recv()

    each_peer(await_slope)

    def adjoint_of(j, total):
        slope = slopes[j]
        by_theta = jnp.where(sub < 4, slope[0:1], slope[4:5])
        by_phi = jnp.where(sub < 4, slope[1:2], slope[5:6])
        tiles = []
        for face in range(2):
            vector = weights[j, 2 * face] * by_theta + weights[j, 2 * face + 1] * by_phi
            turned = -sign * pltpu.roll(vector, 4, 0)
            for y in range(size_y):
                g = face * size_y + y
                tile = vector * phases[j, 0, pl.ds(g, 1), :] + turned * phases[j, 1, pl.ds(g, 1), :]
                tiles.append(jnp.concatenate([tile, -sign * pltpu.roll(tile, 4, 0)], axis=1))
        rows = jnp.concatenate(tiles, axis=0)
        high, low = split(rows)
        both = jnp.concatenate([high, low], axis=0)
        across = (((1,), (1,)), ((), ()))
        by_high = lax.dot_general(both, table_hi[j], across, preferred_element_type=F32)
        by_low = lax.dot_general(high, table_lo[j], across, preferred_element_type=F32)
        return total + by_high[:all_rows] + by_high[all_rows:] + by_low

    gradient = lax.fori_loop(0, chunks, adjoint_of, jnp.zeros((all_rows, size_x + 8 * size_z), F32))
    for y in range(size_y):
        wall = gradient[half_rows + 8 * y : half_rows + 8 * y + 8, size_x:]
        adjoint_out[pl.ds(y, 1), :] = jnp.sum(jnp.where(own_block, wall, 0.0), axis=0, keepdims=True) * norm
        cap = block_transpose(gradient[8 * y : 8 * y + 8, :size_x] * (norm * end_weight))
        adjoint_out[pl.ds(size_y + 8 * y, 8), :] = cap

    for window in range(windows):
        for copy, sends, receives in halo_copies(window):
            @pl.when(sends)
            def _():
                copy.wait_send()
    each_peer(lambda k: part_copy(k).wait_send())

    @pl.when(leads)
    def _():
        each_peer(lambda k: slope_copy(k, chunk).wait_send())

    for k in range(1, slabs):
        wall_copy(k).wait_send()
    for at, holder in enumerate((0, slabs - 1)):
        @pl.when(gz == holder)
        def _():
            for k in range(1, slabs):
                cap_copy(k, at).wait_send()


def local(fields, spectra, permittivity, phase_start, wall_owner, cap_owner, dir_index, target, aim_mask):
    slabs, devs, xys = (lax.axis_size(a) for a in ("gz", "dev", "xy"))
    peers = slabs * devs * xys
    size_y, size_z, size_x = permittivity.shape
    assert size_z == PATCH and size_x == LANES and size_y == 4
    directions = dir_index.shape[0]
    chunks = directions // LANES
    ratio = peers // chunks
    share = directions // peers
    cap_count = size_y * size_x // PATCH
    owned = size_y + 2 * (cap_count // slabs)
    rows = 16 * size_y
    depth = size_x + 8 * size_z
    windows = 2 * STEPS
    vmem, smem = (pl.BlockSpec(memory_space=s) for s in (pltpu.VMEM, pltpu.SMEM))
    dma = pltpu.SemaphoreType.DMA
    outs = pl.pallas_call(
        functools.partial(kernel, (slabs, devs, xys)),
        out_shape=(
            jax.ShapeDtypeStruct(fields.shape, F32),
            jax.ShapeDtypeStruct(spectra.shape, F32),
            jax.ShapeDtypeStruct((owned, LANES), F32),
            jax.ShapeDtypeStruct((1, LANES), F32),
            jax.ShapeDtypeStruct((size_y + cap_count, LANES), F32),
        ),
        in_specs=[vmem, vmem, vmem, smem, smem, vmem, vmem, vmem, vmem],
        out_specs=(vmem,) * 5,
        scratch_shapes=[
            pltpu.VMEM((windows, 2, size_z, LANES), F32),
            pltpu.VMEM((windows, 2, size_y, 1, LANES), F32),
            pltpu.VMEM((windows, size_z, LANES), F32),
            pltpu.VMEM((windows, 2, size_z, LANES), F32),
            pltpu.VMEM((windows, 2, size_y, 1, LANES), F32),
            pltpu.VMEM((windows, size_z, LANES), F32),
            pltpu.VMEM((8, chunks, LANES), F32),
            pltpu.VMEM((chunks, 4, 8, LANES), F32),
            pltpu.VMEM((chunks, 2, 2 * size_y, LANES), F32),
            pltpu.VMEM((chunks, depth, 2 * LANES), BF16),
            pltpu.VMEM((chunks, depth, 2 * LANES), BF16),
            pltpu.VMEM((8 * size_y, LANES), F32),
            pltpu.VMEM((2 * rows, depth), BF16),
            pltpu.VMEM((chunks, 8, LANES), F32),
            pltpu.VMEM((peers, 8, LANES), F32),
            pltpu.VMEM((chunks, 8, LANES), F32),
            pltpu.VMEM((slabs, 8, LANES), F32),
            pltpu.VMEM((2, cap_count, LANES), F32),
            dma((windows, 3)), dma((windows, 3)),
            dma((peers,)), dma((peers,)),
            dma((peers,)), dma((chunks,)),
            dma((slabs,)), dma((slabs,)),
            dma((slabs,)), dma((2,)),
        ],
        compiler_params=pltpu.CompilerParams(collective_id=0, has_side_effects=True),
    )(
        fields, spectra, permittivity, phase_start, wall_owner, cap_owner,
        dir_index.reshape(chunks, LANES), target.reshape(chunks, LANES), aim_mask.reshape(chunks, LANES),
    )
    fields_new, spectra_new, owned_rows, intensity, adjoint = outs
    intensity = intensity.reshape(LANES)
    if ratio > 1:
        me = (lax.axis_index("gz") * devs + lax.axis_index("dev")) * xys + lax.axis_index("xy")
        intensity = lax.dynamic_slice_in_dim(intensity, (me % ratio) * share, share, 0)
    return (fields_new, spectra_new, owned_rows[None, None, None], intensity, adjoint[None, None, None])


def solution(mesh):
    placed = (
        P("groups", "dev", "gz", "xy"),
        P("groups", "dev", "gz", "xy"),
        P(("groups", "dev"), "gz", "xy"),
        P("groups"),
        P("gz", None),
        P(),
        P(),
        P("groups"),
        P("groups"),
    )
    return jax.shard_map(
        local,
        mesh=mesh,
        in_specs=placed,
        out_specs=(
            P("groups", "dev", "gz", "xy"),
            P("groups", "dev", "gz", "xy"),
            P(("groups", "gz"), "dev", "xy", None, None),
            P(("groups", "gz", "dev", "xy")),
            P(("groups", "gz"), "dev", "xy", None, None),
        ),
        check_vma=False,
    )
```

time: 346 us -> 49 us (0.14); the launches traced: 339 us -> 48.7 us
  waiting for transfers between devices: 114 us -> 0 us
  matrix products: 98.6 us -> 0 us
  starting transfers between devices: 49.7 us -> 0 us
  Pallas kernels: 0 us -> 41.8 us
  blocking collectives: 41 us -> 0 us
  between operations: 17 us -> 1.3 us
  local copies, waits for them, and re-layouts: 12.6 us -> 5.6 us
  other arithmetic: 6.95 us -> 0 us
    dot_general x44 -> x0, matrix products: 98.6 us -> none  [the longest x4 12.3 us: adjoint_block(): jnp.dot(slope_block[:6], cosine_table.T, precision=HIGHEST)]
    psum x1 -> x0, waiting for transfers between devices: 85.2 us -> none  [local(): far_total = lax.psum(partial_far, ('gz', 'dev', 'xy'))]
    pallas_call x0 -> x1, Pallas kernels: none -> 41.8 us  [local(): pl.pallas_call(functools.partial(kernel, (slabs, devs, xys)), out_shape=(...]
    psum x2 -> x0, blocking collectives: 41 us -> none  [the longest x1 21.5 us: broadcast(): return lax.psum(block, axis)]
    ppermute x18 -> x0, starting transfers between devices: 33.9 us -> none  [the longest x9 22.3 us: padded_2(): before = lax.ppermute(last, axis, up)]
    ppermute x18 -> x0, waiting for transfers between devices: 28.3 us -> none  [the longest x9 26.8 us: padded_2(): after = lax.ppermute(first, axis, down)]
    all_to_all x3 -> x0, starting transfers between devices: 15.7 us -> none  [the longest x1 6.35 us: local(): lax.all_to_all(send_meta, 'gz', split_axis=0, concat_axis=0, tiled=True)]
  transfers between devices with their start and end apart: 22 -> 0, of which waited for: 12 -> 0; matrix products, arithmetic and copies ran while one was open for 2% -> 0% of each run, Pallas kernels for 0% -> 0%
where the time goes in v1:
time: 49 us; the launch traced here: 48.7 us
  Pallas kernels  41.8 us (85%)
  local copies, waits for them, and re-layouts  5.6 us (11%)
  between operations  1.3 us (3%)
    pallas_call x1, Pallas kernels, local(): pl.pallas_call(functools.partial(kernel, (slabs, devs, xys)), out_shape=(...  41.8 us
    unnamed x9, local copies, waits for them, and re-layouts  5.6 us

profile of v1, /device:TPU:0, one launch (start us, length us, event | category | flops | bytes accessed | tf_op | source)
XLA Modules:
  0.0 48.7 jit_solution(7926185907849715221)
XLA Ops:
  1.3 41.8 %shard_map.128 = (f32[6,4,16,128]{3,2,1,0:T(8,128)}, f32[12,4,16,128]{3,2,1,0:T(8,128)}, f32[20,128]{1,0:T(8,128)}, f32[1,128]{1,0:T(1,128)}, f32[36,128]{1,0:T(8,128)}) custom-call(f32[6,4,16,128]{3,2,1,0:T(8,128)} %fields.1, f32[12,4,16,128]{3,2,1,0:T(8,128)} %spectra.1, f32[4,16,128]{2,1,0:T(8,128)} %permit.1, f32[1]{0:T(128)S(6)} %copy.19.phase, ...), custom_call_target="tpu_custom_call" | custom-call | tf_op jit(solution)/shard_map/pallas_call | solution.py:532
  43.1 0.0 copy-start
  43.1 1.4 %copy.14 = f32[1,1,1,20,128]{4,2,3,1,0:T(1,128)} copy(f32[1,1,1,20,128]{4,3,2,1,0:T(8,128)} %bitcast.7) | data formatting | bytes 20480
  44.5 1.4 %copy.15 = f32[1,1,1,36,128]{4,2,3,1,0:T(1,128)} copy(f32[1,1,1,36,128]{4,3,2,1,0:T(8,128)} %bitcast.6) | data formatting | bytes 36864
  45.8 1.6 %copy.20 = f32[6,4,16,128]{3,2,1,0:T(8,128)} copy(f32[6,4,16,128]{3,2,1,0:T(8,128)} %get-tuple-element.25) | data formatting | bytes 393216
  47.4 0.0 copy-done
  47.5 0.0 copy-start.1
  47.5 0.7 %copy.21 = f32[12,4,16,128]{3,2,1,0:T(8,128)} copy(f32[12,4,16,128]{3,2,1,0:T(8,128)S(1)} %copy-done) | data formatting | bytes 786432
  48.2 0.0 copy-done.1
  48.2 0.5 %copy.22 = f32[128]{0:T(128)} copy(f32[128]{0:T(128)S(1)} %bitcast.11) | data formatting | bytes 1024
Async XLA Ops:
  43.1 4.3 %copy-start = (f32[12,4,16,128]{3,2,1,0:T(8,128)S(1)}, f32[12,4,16,128]{3,2,1,0:T(8,128)}, u32[]{:S(2)}) copy-start(f32[12,4,16,128]{3,2,1,0:T(8,128)} %get-tuple-element.26) | copy-start | bytes 1179652
  47.5 0.8 %copy-start.1 = (f32[1,128]{1,0:T(1,128)S(1)}, f32[1,128]{1,0:T(1,128)}, u32[]{:S(2)}) copy-start(f32[1,128]{1,0:T(1,128)} %get-tuple-element.13) | copy-start | bytes 1540

commit v2 on v1

--- a/solution.py
+++ b/solution.py
@@ -55,12 +55,12 @@
 
 def kernel(
     sizes,
-    fields, spectra, permit, phase, wall_owner, cap_owner, dirs, target, aim,
+    fields_in, spectra_in, permit_in, phase, wall_owner, cap_owner, dirs, target, aim,
     fields_out, spectra_out, owned_out, intensity_out, adjoint_out,
     send_y, send_z, send_x, got_y, got_z, got_x,
-    geo, weights, phases, table_hi, table_lo, cap_plane, lhs,
+    fields, spectra, permit, geo, weights, phases, table_hi, table_lo, cap_plane, lhs,
     parts_out, parts_in, slopes, walls, caps,
-    halo_send, halo_got, part_send, part_got, slope_send, slope_got, wall_send, wall_got, cap_send, cap_got,
+    halo_send, halo_got, part_send, part_got, slope_send, slope_got, wall_send, wall_got, cap_send, cap_got, loads,
 ):
     slabs, devs, xys = sizes
     peers = slabs * devs * xys
@@ -74,6 +74,13 @@
     me = (gz * devs + dev) * xys + xy
     place = {"dev": dev, "gz": gz, "xy": xy}
     count = {"dev": devs, "gz": slabs, "xy": xys}
+
+    loading = [
+        pltpu.make_async_copy(source, held, loads.at[number])
+        for number, (source, held) in enumerate(((fields_in, fields), (permit_in, permit), (spectra_in, spectra)))
+    ]
+    for copy in loading:
+        copy.start()
 
     def ident(flat):
         return {"gz": flat // (devs * xys), "dev": (flat // xys) % devs, "xy": flat % xys}
@@ -167,6 +174,7 @@
             for window in range(1, windows, 2):
                 got[window] = jnp.zeros(got.shape[1:], F32)
 
+    loading[0].wait()
     pl.semaphore_wait(barrier, peers - 1)
 
     lane = iota((size_z, LANES), 1)
@@ -249,7 +257,9 @@
 
     ex, ey, ez = fields[0], fields[1], fields[2]
     start_halo(0, (ez, ex), (ey, ex), (ez, ey))
+    loading[1].wait()
     rate = COURANT / permit[...]
+    loading[2].wait()
     hx, hy, hz = fields[3], fields[4], fields[5]
     spec_from = spectra
     for n in range(STEPS):
@@ -310,9 +320,51 @@
             lhs[pl.ds(first, 8), :] = jnp.concatenate([cap_part, none], axis=1)
             lhs[pl.ds(first + half_rows, 8), :] = jnp.concatenate([none, wall_part], axis=1)
 
+    lanes8 = iota((1, LANES), 1)
+    owner_row = jnp.zeros((1, LANES), F32)
+    for p in range(size_y):
+        owner_row = jnp.where(lanes8 == 8 * gz + p, (wall_owner[0, p] + 1).astype(F32), owner_row)
+    own_walls[pl.ds(size_y, 1), :] = owner_row
+
+    def wall_copy(k):
+        return pltpu.make_async_remote_copy(
+            src_ref=walls.at[gz],
+            dst_ref=walls.at[gz],
+            send_sem=wall_send.at[k],
+            recv_sem=wall_got.at[gz],
+            device_id={"gz": (gz + k) % slabs},
+            device_id_type=MESH,
+        )
+
+    def wall_landing(s):
+        return pltpu.make_async_remote_copy(
+            src_ref=walls.at[s], dst_ref=walls.at[s], send_sem=wall_send.at[0], recv_sem=wall_got.at[s],
+            device_id={"gz": (gz + 1) % slabs}, device_id_type=MESH,
+        )
+
+    def cap_copy(k, at):
+        return pltpu.make_async_remote_copy(
+            src_ref=caps.at[at],
+            dst_ref=caps.at[at],
+            send_sem=cap_send.at[k],
+            recv_sem=cap_got.at[at],
+            device_id={"gz": (gz + k) % slabs},
+            device_id_type=MESH,
+        )
+
+    for k in range(1, slabs):
+        wall_copy(k).start()
+    for at, holder in enumerate((0, slabs - 1)):
+        @pl.when(gz == holder)
+        def _():
+            for y in range(size_y):
+                caps[at, pl.ds(8 * y, 8), :] = block_transpose(cap_plane[pl.ds(8 * y, 8), :])
+            for k in range(1, slabs):
+                cap_copy(k, at).start()
+
     sign = jnp.where(sub < 4, -1.0, 1.0)
 
-    def far_of(j, carry):
+    def far_of(j):
         rows = lhs[...]
         by_high = jnp.dot(rows, table_hi[j], preferred_element_type=F32)
         by_low = jnp.dot(rows[:all_rows], table_lo[j], preferred_element_type=F32)
@@ -337,9 +389,15 @@
             return pairs + pltpu.roll(pairs, 6, 0)
 
         parts_out[j] = jnp.where(sub % 4 == 1, pltpu.roll(four(phi), 1, 0), four(theta))
-        return carry
-
-    lax.fori_loop(0, chunks, far_of, 0)
+
+    chunk = me // ratio
+
+    def partner(number):
+        other, bit = 0, 1
+        while bit < chunks:
+            other = other + bit * ((chunk // bit + number // bit) % 2)
+            bit *= 2
+        return other
 
     def part_copy(k):
         peer = (me + k) % peers
@@ -359,54 +417,52 @@
 
         lax.fori_loop(1, peers, body, 0)
 
-    each_peer(lambda k: part_copy(k).start())
-
-    lanes8 = iota((1, LANES), 1)
-    owner_row = jnp.zeros((1, LANES), F32)
-    for p in range(size_y):
-        owner_row = jnp.where(lanes8 == 8 * gz + p, (wall_owner[0, p] + 1).astype(F32), owner_row)
-    own_walls[pl.ds(size_y, 1), :] = owner_row
-
-    def wall_copy(k):
-        return pltpu.make_async_remote_copy(
-            src_ref=walls.at[gz],
-            dst_ref=walls.at[gz],
-            send_sem=wall_send.at[k],
-            recv_sem=wall_got.at[gz],
-            device_id={"gz": (gz + k) % slabs},
-            device_id_type=MESH,
+    def far_and_send(number, carry):
+        to = partner(chunks - 1 - number)
+        far_of(to)
+        for r in range(ratio):
+            peer = to * ratio + r
+
+            @pl.when(peer != me)
+            def _():
+                part_copy((peer - me + peers) % peers).start()
+
+        return carry
+
+    lax.fori_loop(0, chunks, far_and_send, 0)
+    parts_in[0] = parts_out[chunk]
+
+    for s in range(slabs):
+        @pl.when(s != gz)
+        def _():
+            wall_landing(s).wait_recv()
+    for at, holder in enumerate((0, slabs - 1)):
+        @pl.when(gz != holder)
+        def _():
+            cap_copy(1, at).wait_recv()
+
+    def choose(mine, share, records):
+        length = mine.shape[1]
+        before = jnp.where(iota((length, length), 0) < iota((length, length), 1), 1.0, 0.0).astype(BF16)
+        ones = jnp.broadcast_to(jnp.where(mine, 1.0, 0.0), (8, length))
+        rank = jnp.dot(ones.astype(BF16), before, preferred_element_type=F32)
+        wanted = iota((8, length), 0).astype(F32)
+        chooser = jnp.where(rank == wanted, ones, 0.0)
+        return jnp.dot(chooser, records, precision=HIGHEST, preferred_element_type=F32)[:share]
+
+    all_walls = walls[...]
+    owner_all = jnp.sum(all_walls[:, size_y : size_y + 1, :], axis=0)[:, : 8 * slabs]
+    cap_share = (owned_out.shape[0] - size_y) // 2
+    owned_out[pl.ds(0, size_y), 0, :] = choose(
+        owner_all == (gz + 1).astype(F32), size_y, all_walls.reshape(8 * slabs, LANES)
+    )
+    for at in range(2):
+        owned_out[pl.ds(size_y + at * cap_share, cap_share), 0, :] = choose(
+            cap_owner[pl.ds(at, 1), :] == gz, cap_share, caps[at]
         )
 
-    def wall_landing(s):
-        return pltpu.make_async_remote_copy(
-            src_ref=walls.at[s], dst_ref=walls.at[s], send_sem=wall_send.at[0], recv_sem=wall_got.at[s],
-            device_id={"gz": (gz + 1) % slabs}, device_id_type=MESH,
-        )
-
-    def cap_copy(k, at):
-        return pltpu.make_async_remote_copy(
-            src_ref=caps.at[at],
-            dst_ref=caps.at[at],
-            send_sem=cap_send.at[k],
-            recv_sem=cap_got.at[at],
-            device_id={"gz": (gz + k) % slabs},
-            device_id_type=MESH,
-        )
-
-    for k in range(1, slabs):
-        wall_copy(k).start()
-    for at, holder in enumerate((0, slabs - 1)):
-        @pl.when(gz == holder)
-        def _():
-            for y in range(size_y):
-                caps[at, pl.ds(8 * y, 8), :] = block_transpose(cap_plane[pl.ds(8 * y, 8), :])
-            for k in range(1, slabs):
-                cap_copy(k, at).start()
-
-    parts_in[0] = parts_out[me // ratio]
     each_peer(lambda k: part_copy(k).wait_recv())
     field = jnp.sum(parts_in[...], axis=0)
-    chunk = me // ratio
     power = jnp.where(sub % 4 < 2, field * field, 0.0)
     intensity = jnp.sum(power, axis=0, keepdims=True)
     intensity_out[...] = intensity
@@ -428,45 +484,13 @@
         slopes[chunk] = 2.0 * residual * field
         each_peer(lambda k: slope_copy(k, chunk).start())
 
-    for s in range(slabs):
-        @pl.when(s != gz)
+    def adjoint_of(number, total):
+        j = partner(number)
+
+        @pl.when(j * ratio != me)
         def _():
-            wall_landing(s).wait_recv()
-    for at, holder in enumerate((0, slabs - 1)):
-        @pl.when(gz != holder)
-        def _():
-            cap_copy(1, at).wait_recv()
-
-    def choose(mine, share, records):
-        length = mine.shape[1]
-        before = jnp.where(iota((length, length), 0) < iota((length, length), 1), 1.0, 0.0).astype(BF16)
-        ones = jnp.broadcast_to(jnp.where(mine, 1.0, 0.0), (8, length))
-        rank = jnp.dot(ones.astype(BF16), before, preferred_element_type=F32)
-        wanted = iota((8, length), 0).astype(F32)
-        chooser = jnp.where(rank == wanted, ones, 0.0)
-        return jnp.dot(chooser, records, precision=HIGHEST, preferred_element_type=F32)[:share]
-
-    all_walls = walls[...]
-    owner_all = jnp.sum(all_walls[:, size_y : size_y + 1, :], axis=0)[:, : 8 * slabs]
-    cap_share = (owned_out.shape[0] - size_y) // 2
-    owned_out[pl.ds(0, size_y), :] = choose(
-        owner_all == (gz + 1).astype(F32), size_y, all_walls.reshape(8 * slabs, LANES)
-    )
-    for at in range(2):
-        owned_out[pl.ds(size_y + at * cap_share, cap_share), :] = choose(
-            cap_owner[pl.ds(at, 1), :] == gz, cap_share, caps[at]
-        )
-
-    def await_slope(k):
-        sender = (me + peers - k) % peers
-
-        @pl.when(sender % ratio == 0)
-        def _():
-            slope_copy(1, sender // ratio).wait_recv()
-
-    each_peer(await_slope)
-
-    def adjoint_of(j, total):
+            slope_copy(1, j).wait_recv()
+
         slope = slopes[j]
         by_theta = jnp.where(sub < 4, slope[0:1], slope[4:5])
         by_phi = jnp.where(sub < 4, slope[1:2], slope[5:6])
@@ -489,9 +513,9 @@
     gradient = lax.fori_loop(0, chunks, adjoint_of, jnp.zeros((all_rows, size_x + 8 * size_z), F32))
     for y in range(size_y):
         wall = gradient[half_rows + 8 * y : half_rows + 8 * y + 8, size_x:]
-        adjoint_out[pl.ds(y, 1), :] = jnp.sum(jnp.where(own_block, wall, 0.0), axis=0, keepdims=True) * norm
+        adjoint_out[pl.ds(y, 1), 0, :] = jnp.sum(jnp.where(own_block, wall, 0.0), axis=0, keepdims=True) * norm
         cap = block_transpose(gradient[8 * y : 8 * y + 8, :size_x] * (norm * end_weight))
-        adjoint_out[pl.ds(size_y + 8 * y, 8), :] = cap
+        adjoint_out[pl.ds(size_y + 8 * y, 8), 0, :] = cap
 
     for window in range(windows):
         for copy, sends, receives in halo_copies(window):
@@ -511,6 +535,14 @@
         def _():
             for k in range(1, slabs):
                 cap_copy(k, at).wait_send()
+
+
+def write_out(*refs):
+    copies = [pltpu.make_async_copy(refs[i], refs[5 + i], refs[10].at[i]) for i in range(5)]
+    for copy in copies:
+        copy.start()
+    for copy in copies:
+        copy.wait()
 
 
 def local(fields, spectra, permittivity, phase_start, wall_owner, cap_owner, dir_index, target, aim_mask):
@@ -528,17 +560,18 @@
     depth = size_x + 8 * size_z
     windows = 2 * STEPS
     vmem, smem = (pl.BlockSpec(memory_space=s) for s in (pltpu.VMEM, pltpu.SMEM))
+    anywhere = pl.BlockSpec(memory_space=pl.ANY)
     dma = pltpu.SemaphoreType.DMA
     outs = pl.pallas_call(
         functools.partial(kernel, (slabs, devs, xys)),
         out_shape=(
-            jax.ShapeDtypeStruct(fields.shape, F32),
-            jax.ShapeDtypeStruct(spectra.shape, F32),
-            jax.ShapeDtypeStruct((owned, LANES), F32),
-            jax.ShapeDtypeStruct((1, LANES), F32),
-            jax.ShapeDtypeStruct((size_y + cap_count, LANES), F32),
+            pltpu.VMEM(fields.shape, F32),
+            pltpu.VMEM(spectra.shape, F32),
+            pltpu.VMEM((owned, 1, LANES), F32),
+            pltpu.VMEM((1, LANES), F32),
+            pltpu.VMEM((size_y + cap_count, 1, LANES), F32),
         ),
-        in_specs=[vmem, vmem, vmem, smem, smem, vmem, vmem, vmem, vmem],
+        in_specs=[anywhere, anywhere, anywhere, smem, smem, vmem, vmem, vmem, vmem],
         out_specs=(vmem,) * 5,
         scratch_shapes=[
             pltpu.VMEM((windows, 2, size_z, LANES), F32),
@@ -547,6 +580,9 @@
             pltpu.VMEM((windows, 2, size_z, LANES), F32),
             pltpu.VMEM((windows, 2, size_y, 1, LANES), F32),
             pltpu.VMEM((windows, size_z, LANES), F32),
+            pltpu.VMEM(fields.shape, F32),
+            pltpu.VMEM(spectra.shape, F32),
+            pltpu.VMEM(permittivity.shape, F32),
             pltpu.VMEM((8, chunks, LANES), F32),
             pltpu.VMEM((chunks, 4, 8, LANES), F32),
             pltpu.VMEM((chunks, 2, 2 * size_y, LANES), F32),
@@ -564,18 +600,28 @@
             dma((peers,)), dma((chunks,)),
             dma((slabs,)), dma((slabs,)),
             dma((slabs,)), dma((2,)),
+            dma((3,)),
         ],
         compiler_params=pltpu.CompilerParams(collective_id=0, has_side_effects=True),
     )(
         fields, spectra, permittivity, phase_start, wall_owner, cap_owner,
         dir_index.reshape(chunks, LANES), target.reshape(chunks, LANES), aim_mask.reshape(chunks, LANES),
     )
-    fields_new, spectra_new, owned_rows, intensity, adjoint = outs
+    held = (fields.shape, spectra.shape, (owned, 1, LANES), (1, LANES), (size_y + cap_count, 1, LANES))
+    fields_new, spectra_new, owned_rows, intensity, adjoint = pl.pallas_call(
+        write_out,
+        out_shape=tuple(jax.ShapeDtypeStruct(shape, F32) for shape in held),
+        in_specs=[pl.BlockSpec(memory_space=pltpu.VMEM)] * 5,
+        out_specs=(pl.BlockSpec(memory_space=pl.ANY),) * 5,
+        scratch_shapes=[dma((5,))],
+    )(*(pltpu.with_memory_space_constraint(out, pltpu.VMEM) for out in outs))
+    owned_rows = owned_rows.reshape(1, 1, owned, 1, LANES).transpose(0, 1, 3, 2, 4)
+    adjoint = adjoint.reshape(1, 1, size_y + cap_count, 1, LANES).transpose(0, 1, 3, 2, 4)
     intensity = intensity.reshape(LANES)
     if ratio > 1:
         me = (lax.axis_index("gz") * devs + lax.axis_index("dev")) * xys + lax.axis_index("xy")
         intensity = lax.dynamic_slice_in_dim(intensity, (me % ratio) * share, share, 0)
-    return (fields_new, spectra_new, owned_rows[None, None, None], intensity, adjoint[None, None, None])
+    return (fields_new, spectra_new, owned_rows, intensity, adjoint)
 
 
 def solution(mesh):

time: 49 us -> 39.6 us (0.81)
  local copies, waits for them, and re-layouts: 5.6 us -> 0 us
  Pallas kernels: 41.8 us -> 38.1 us
    unnamed x9 -> x0, local copies, waits for them, and re-layouts: 5.6 us -> none
    pallas_call x1, Pallas kernels: 41.8 us -> 37.2 us  [local(): pl.pallas_call(functools.partial(kernel, (slabs, devs, xys)), out_shape=(...]
    pallas_call x0 -> x1, Pallas kernels: none -> 0.86 us  [local(): pl.pallas_call(write_out, out_shape=tuple((jax.ShapeDtypeStruct(shape, F3...]
where the time goes in v2:
time: 39.6 us; the launch traced here: 39.4 us
  Pallas kernels  38.1 us (96%)
  between operations  1.29 us (3%)
    pallas_call x1, Pallas kernels, local(): pl.pallas_call(functools.partial(kernel, (slabs, devs, xys)), out_shape=(...  37.2 us
    pallas_call x1, Pallas kernels, local(): pl.pallas_call(write_out, out_shape=tuple((jax.ShapeDtypeStruct(shape, F3...  0.86 us

profile of v2, /device:TPU:0, one launch (start us, length us, event | category | flops | bytes accessed | tf_op | source)
XLA Modules:
  0.0 39.4 jit_solution(2763382956325541720)
XLA Ops:
  1.3 37.2 %shard_map.128 = (f32[6,4,16,128]{3,2,1,0:T(8,128)S(1)}, f32[12,4,16,128]{3,2,1,0:T(8,128)S(1)}, f32[20,1,128]{2,1,0:T(1,128)S(1)}, f32[1,128]{1,0:T(1,128)S(1)}, f32[36,1,128]{2,1,0:T(1,128)S(1)}) custom-call(f32[6,4,16,128]{3,2,1,0:T(8,128)} %fields_in.1, f32[12,4,16,128]{3,2,1,0:T(8,128)} %spectra_in.1, f32[4,16,128]{2,1,0:T(8,128)} %permit_in.1, ...), custom_call_target="tpu_custom_call" | custom-call | tf_op jit(solution)/shard_map/pallas_call | solution.py:565
  38.5 0.9 %shard_map.129 = (f32[6,4,16,128]{3,2,1,0:T(8,128)}, f32[12,4,16,128]{3,2,1,0:T(8,128)}, f32[20,1,128]{2,1,0:T(1,128)}, f32[1,128]{1,0:T(1,128)}, f32[36,1,128]{2,1,0:T(1,128)}) custom-call(f32[6,4,16,128]{3,2,1,0:T(8,128)S(1)} %get-tuple-element.15.refs_0_, f32[12,4,16,128]{3,2,1,0:T(8,128)S(1)} %get-tuple-element.16.refs_1_, ...), custom_call_target="tpu_custom_call" | custom-call | tf_op jit(solution)/shard_map/pallas_call | solution.py:611

commit v3 on v2

--- a/solution.py
+++ b/solution.py
@@ -161,7 +161,7 @@
         lax.fori_loop(window * chunks // windows, (window + 1) * chunks // windows, make_tables, 0)
 
     order = iota((8, LANES), 0).astype(F32)
-    run_s, run_c = sincos((phase[0] + 0.5 * ANGULAR_STEP * (order + 1.0)) * (0.5 / math.pi))
+    run_s, run_c = sincos((phase[...] + 0.5 * ANGULAR_STEP * (order + 1.0)) * (0.5 / math.pi))
 
     for number, (axis, got) in enumerate(zip(AXES, (got_y, got_z, got_x))):
         @pl.when(place[axis] == count[axis] - 1)
@@ -208,6 +208,11 @@
         for k in range(2):
             send_y[window, k] = for_y[k][at_y]
             send_z[window, k] = for_z[k][:, at_z : at_z + 1, :]
+        copies = halo_copies(window)
+        for copy, sends, receives in copies[:2]:
+            @pl.when(sends)
+            def _():
+                copy.start()
         packed = jnp.zeros((size_z, LANES), F32)
         for k in range(2):
             for y in range(size_y):
@@ -217,10 +222,11 @@
                 turned = pltpu.roll(value, amount, 1) if amount else value
                 packed = jnp.where(lane == spot, turned, packed)
         send_x[window] = packed
-        for copy, sends, receives in halo_copies(window):
-            @pl.when(sends)
-            def _():
-                copy.start()
+        copy, sends, receives = copies[2]
+
+        @pl.when(sends)
+        def _():
+            copy.start()
 
     def wait_halo(window):
         for copy, sends, receives in halo_copies(window):
@@ -228,32 +234,34 @@
             def _():
                 copy.wait_recv()
 
-    def shift_y(window, k, value):
+    def inner(ahead, axis, value):
+        if axis == 0:
+            none = jnp.zeros_like(value[:1])
+            if ahead:
+                return jnp.concatenate([value[1:], none], axis=0) - value
+            return value - jnp.concatenate([none, value[:-1]], axis=0)
+        length = value.shape[axis]
+        spots = row3 if axis == 1 else lane3
+        if ahead:
+            return jnp.where(spots == length - 1, 0.0, pltpu.roll(value, length - 1, axis)) - value
+        return value - jnp.where(spots == 0, 0.0, pltpu.roll(value, 1, axis))
+
+    def edge_y(window, k):
         other = got_y[window, k][None]
-        if window % 2 == 0:
-            return jnp.concatenate([value[1:], other], axis=0) - value
-        return value - jnp.concatenate([other, value[:-1]], axis=0)
-
-    def shift_z(window, k, value):
-        other = got_z[window, k]
-        if window % 2 == 0:
-            return jnp.where(row3 == size_z - 1, other, pltpu.roll(value, size_z - 1, 1)) - value
-        return value - jnp.where(row3 == 0, other, pltpu.roll(value, 1, 1))
-
-    def shift_x(window, k, value):
+        none = jnp.zeros((size_y - 1, size_z, LANES), F32)
+        return jnp.concatenate([none, other] if window % 2 == 0 else [other, none], axis=0)
+
+    def edge_z(window, k):
+        return jnp.where(row3 == (size_z - 1 if window % 2 == 0 else 0), got_z[window, k], 0.0)
+
+    def edge_x(window, k):
         landed = got_x[window]
         edges = []
         for y in range(size_y):
             spot = k * size_y + y
-            if window % 2 == 0:
-                edges.append(pltpu.roll(landed, LANES - 1 - spot, 1))
-            else:
-                amount = (LANES - spot) % LANES
-                edges.append(pltpu.roll(landed, amount, 1) if amount else landed)
-        other = jnp.stack(edges, axis=0)
-        if window % 2 == 0:
-            return jnp.where(lane3 == size_x - 1, other, pltpu.roll(value, size_x - 1, 2)) - value
-        return value - jnp.where(lane3 == 0, other, pltpu.roll(value, 1, 2))
+            amount = (LANES - 1 - spot) if window % 2 == 0 else (LANES - spot) % LANES
+            edges.append(pltpu.roll(landed, amount, 1) if amount else landed)
+        return jnp.where(lane3 == (size_x - 1 if window % 2 == 0 else 0), jnp.stack(edges, axis=0), 0.0)
 
     ex, ey, ez = fields[0], fields[1], fields[2]
     start_halo(0, (ez, ex), (ey, ex), (ez, ey))
@@ -264,22 +272,28 @@
     spec_from = spectra
     for n in range(STEPS):
         window = 2 * n
+        hx = hx - COURANT * (inner(True, 0, ez) - inner(True, 1, ey))
+        hy = hy - COURANT * (inner(True, 1, ex) - inner(True, 2, ez))
+        hz = hz - COURANT * (inner(True, 2, ey) - inner(True, 0, ex))
         tables_of(window)
         wait_halo(window)
-        hx = hx - COURANT * (shift_y(window, 0, ez) - shift_z(window, 0, ey))
-        hy = hy - COURANT * (shift_z(window, 1, ex) - shift_x(window, 0, ez))
-        hz = hz - COURANT * (shift_x(window, 1, ey) - shift_y(window, 1, ex))
+        hx = hx - COURANT * (edge_y(window, 0) - edge_z(window, 0))
+        hy = hy - COURANT * (edge_z(window, 1) - edge_x(window, 0))
+        hz = hz - COURANT * (edge_x(window, 1) - edge_y(window, 1))
         window = 2 * n + 1
         start_halo(window, (hz, hx), (hy, hx), (hz, hy))
         half_c, half_s = run_c[2 * n : 2 * n + 1, :], run_s[2 * n : 2 * n + 1, :]
         for c, value in enumerate((hx, hy, hz)):
             spectra_out[3 + c] = spec_from[3 + c] + value * half_c
             spectra_out[9 + c] = spec_from[9 + c] - value * half_s
+        ex = ex + rate * (inner(False, 0, hz) - inner(False, 1, hy))
+        ey = ey + rate * (inner(False, 1, hx) - inner(False, 2, hz))
+        ez = ez + rate * (inner(False, 2, hy) - inner(False, 0, hx))
         tables_of(window)
         wait_halo(window)
-        ex = ex + rate * (shift_y(window, 0, hz) - shift_z(window, 0, hy))
-        ey = ey + rate * (shift_z(window, 1, hx) - shift_x(window, 0, hz))
-        ez = ez + rate * (shift_x(window, 1, hy) - shift_y(window, 1, hx))
+        ex = ex - rate * (edge_y(window, 0) - edge_z(window, 0))
+        ey = ey - rate * (edge_z(window, 1) - edge_x(window, 0))
+        ez = ez - rate * (edge_x(window, 1) - edge_y(window, 1))
         if n < STEPS - 1:
             start_halo(window + 1, (ez, ex), (ey, ex), (ez, ey))
         full_c, full_s = run_c[2 * n + 1 : 2 * n + 2, :], run_s[2 * n + 1 : 2 * n + 2, :]
@@ -392,6 +406,8 @@
 
     chunk = me // ratio
 
+    bunch = 4 if chunks % 4 == 0 else 1
+
     def partner(number):
         other, bit = 0, 1
         while bit < chunks:
@@ -418,18 +434,24 @@
         lax.fori_loop(1, peers, body, 0)
 
     def far_and_send(number, carry):
-        to = partner(chunks - 1 - number)
-        far_of(to)
-        for r in range(ratio):
-            peer = to * ratio + r
+        several = [partner(chunks - 1 - bunch * number - m) for m in range(bunch)]
+        for to in several:
+            far_of(to)
+
+        def send(m, inner_carry):
+            to = partner(chunks - 1 - bunch * number - m // ratio)
+            peer = to * ratio + m % ratio
 
             @pl.when(peer != me)
             def _():
                 part_copy((peer - me + peers) % peers).start()
 
+            return inner_carry
+
+        lax.fori_loop(0, bunch * ratio, send, 0)
         return carry
 
-    lax.fori_loop(0, chunks, far_and_send, 0)
+    lax.fori_loop(0, chunks // bunch, far_and_send, 0)
     parts_in[0] = parts_out[chunk]
 
     for s in range(slabs):
@@ -484,13 +506,7 @@
         slopes[chunk] = 2.0 * residual * field
         each_peer(lambda k: slope_copy(k, chunk).start())
 
-    def adjoint_of(number, total):
-        j = partner(number)
-
-        @pl.when(j * ratio != me)
-        def _():
-            slope_copy(1, j).wait_recv()
-
+    def adjoint_of(j):
         slope = slopes[j]
         by_theta = jnp.where(sub < 4, slope[0:1], slope[4:5])
         by_phi = jnp.where(sub < 4, slope[1:2], slope[5:6])
@@ -508,9 +524,20 @@
         across = (((1,), (1,)), ((), ()))
         by_high = lax.dot_general(both, table_hi[j], across, preferred_element_type=F32)
         by_low = lax.dot_general(high, table_lo[j], across, preferred_element_type=F32)
-        return total + by_high[:all_rows] + by_high[all_rows:] + by_low
-
-    gradient = lax.fori_loop(0, chunks, adjoint_of, jnp.zeros((all_rows, size_x + 8 * size_z), F32))
+        return by_high[:all_rows] + by_high[all_rows:] + by_low
+
+    def adjoint_some(number, total):
+        several = [partner(bunch * number + m) for m in range(bunch)]
+        for j in several:
+            @pl.when(j * ratio != me)
+            def _():
+                slope_copy(1, j).wait_recv()
+
+        for j in several:
+            total = total + adjoint_of(j)
+        return total
+
+    gradient = lax.fori_loop(0, chunks // bunch, adjoint_some, jnp.zeros((all_rows, size_x + 8 * size_z), F32))
     for y in range(size_y):
         wall = gradient[half_rows + 8 * y : half_rows + 8 * y + 8, size_x:]
         adjoint_out[pl.ds(y, 1), 0, :] = jnp.sum(jnp.where(own_block, wall, 0.0), axis=0, keepdims=True) * norm
@@ -571,7 +598,7 @@
             pltpu.VMEM((1, LANES), F32),
             pltpu.VMEM((size_y + cap_count, 1, LANES), F32),
         ),
-        in_specs=[anywhere, anywhere, anywhere, smem, smem, vmem, vmem, vmem, vmem],
+        in_specs=[anywhere, anywhere, anywhere, vmem, smem, vmem, vmem, vmem, vmem],
         out_specs=(vmem,) * 5,
         scratch_shapes=[
             pltpu.VMEM((windows, 2, size_z, LANES), F32),
@@ -604,7 +631,7 @@
         ],
         compiler_params=pltpu.CompilerParams(collective_id=0, has_side_effects=True),
     )(
-        fields, spectra, permittivity, phase_start, wall_owner, cap_owner,
+        fields, spectra, permittivity, phase_start.reshape(1, 1), wall_owner, cap_owner,
         dir_index.reshape(chunks, LANES), target.reshape(chunks, LANES), aim_mask.reshape(chunks, LANES),
     )
     held = (fields.shape, spectra.shape, (owned, 1, LANES), (1, LANES), (size_y + cap_count, 1, LANES))

time: 39.6 us -> 37 us (0.934)
  Pallas kernels: 38.1 us -> 35.5 us
    pallas_call x1, Pallas kernels: 37.2 us -> 34.6 us  [local(): pl.pallas_call(functools.partial(kernel, (slabs, devs, xys)), out_shape=(...]
where the time goes in v3:
time: 37 us; the launch traced here: 36.8 us
  Pallas kernels  35.5 us (96%)
  between operations  1.29 us (3%)
    pallas_call x1, Pallas kernels, local(): pl.pallas_call(functools.partial(kernel, (slabs, devs, xys)), out_shape=(...  34.6 us
    pallas_call x1, Pallas kernels, local(): pl.pallas_call(write_out, out_shape=tuple((jax.ShapeDtypeStruct(shape, F3...  0.86 us

profile of v3, /device:TPU:0, one launch (start us, length us, event | category | flops | bytes accessed | tf_op | source)
XLA Modules:
  0.0 36.8 jit_solution(8351632898770172780)
XLA Ops:
  1.3 34.6 %shard_map.128 = (f32[6,4,16,128]{3,2,1,0:T(8,128)S(1)}, f32[12,4,16,128]{3,2,1,0:T(8,128)S(1)}, f32[20,1,128]{2,1,0:T(1,128)S(1)}, f32[1,128]{1,0:T(1,128)S(1)}, f32[36,1,128]{2,1,0:T(1,128)S(1)}) custom-call(f32[6,4,16,128]{3,2,1,0:T(8,128)} %fields_in.1, f32[12,4,16,128]{3,2,1,0:T(8,128)} %spectra_in.1, f32[4,16,128]{2,1,0:T(8,128)} %permit_in.1, ...), custom_call_target="tpu_custom_call" | custom-call | tf_op jit(solution)/shard_map/pallas_call | solution.py:592
  35.9 0.9 %shard_map.129 = (f32[6,4,16,128]{3,2,1,0:T(8,128)}, f32[12,4,16,128]{3,2,1,0:T(8,128)}, f32[20,1,128]{2,1,0:T(1,128)}, f32[1,128]{1,0:T(1,128)}, f32[36,1,128]{2,1,0:T(1,128)}) custom-call(f32[6,4,16,128]{3,2,1,0:T(8,128)S(1)} %get-tuple-element.15.refs_0_, f32[12,4,16,128]{3,2,1,0:T(8,128)S(1)} %get-tuple-element.16.refs_1_, ...), custom_call_target="tpu_custom_call" | custom-call | tf_op jit(solution)/shard_map/pallas_call | solution.py:638

commit v4 on v3

--- a/solution.py
+++ b/solution.py
@@ -506,6 +506,21 @@
         slopes[chunk] = 2.0 * residual * field
         each_peer(lambda k: slope_copy(k, chunk).start())
 
+    for window in range(windows):
+        for copy, sends, receives in halo_copies(window):
+            @pl.when(sends)
+            def _():
+                copy.wait_send()
+    each_peer(lambda k: part_copy(k).wait_send())
+
+    for k in range(1, slabs):
+        wall_copy(k).wait_send()
+    for at, holder in enumerate((0, slabs - 1)):
+        @pl.when(gz == holder)
+        def _():
+            for k in range(1, slabs):
+                cap_copy(k, at).wait_send()
+
     def adjoint_of(j):
         slope = slopes[j]
         by_theta = jnp.where(sub < 4, slope[0:1], slope[4:5])
@@ -544,24 +559,9 @@
         cap = block_transpose(gradient[8 * y : 8 * y + 8, :size_x] * (norm * end_weight))
         adjoint_out[pl.ds(size_y + 8 * y, 8), 0, :] = cap
 
-    for window in range(windows):
-        for copy, sends, receives in halo_copies(window):
-            @pl.when(sends)
-            def _():
-                copy.wait_send()
-    each_peer(lambda k: part_copy(k).wait_send())
-
     @pl.when(leads)
     def _():
         each_peer(lambda k: slope_copy(k, chunk).wait_send())
-
-    for k in range(1, slabs):
-        wall_copy(k).wait_send()
-    for at, holder in enumerate((0, slabs - 1)):
-        @pl.when(gz == holder)
-        def _():
-            for k in range(1, slabs):
-                cap_copy(k, at).wait_send()
 
 
 def write_out(*refs):

time: 37 us -> 36.9 us (level)
  no operation moved by 1% of the time
where the time goes in v4:
time: 36.9 us; the launch traced here: 36.6 us
  Pallas kernels  35.4 us (96%)
  between operations  1.29 us (3%)
    pallas_call x1, Pallas kernels, local(): pl.pallas_call(functools.partial(kernel, (slabs, devs, xys)), out_shape=(...  34.5 us
    pallas_call x1, Pallas kernels, local(): pl.pallas_call(write_out, out_shape=tuple((jax.ShapeDtypeStruct(shape, F3...  0.86 us

profile of v4, /device:TPU:0, one launch (start us, length us, event | category | flops | bytes accessed | tf_op | source)
XLA Modules:
  0.0 36.6 jit_solution(6658765444113564900)
XLA Ops:
  1.3 34.5 %shard_map.128 = (f32[6,4,16,128]{3,2,1,0:T(8,128)S(1)}, f32[12,4,16,128]{3,2,1,0:T(8,128)S(1)}, f32[20,1,128]{2,1,0:T(1,128)S(1)}, f32[1,128]{1,0:T(1,128)S(1)}, f32[36,1,128]{2,1,0:T(1,128)S(1)}) custom-call(f32[6,4,16,128]{3,2,1,0:T(8,128)} %fields_in.1, f32[12,4,16,128]{3,2,1,0:T(8,128)} %spectra_in.1, f32[4,16,128]{2,1,0:T(8,128)} %permit_in.1, ...), custom_call_target="tpu_custom_call" | custom-call | tf_op jit(solution)/shard_map/pallas_call | solution.py:592
  35.8 0.9 %shard_map.129 = (f32[6,4,16,128]{3,2,1,0:T(8,128)}, f32[12,4,16,128]{3,2,1,0:T(8,128)}, f32[20,1,128]{2,1,0:T(1,128)}, f32[1,128]{1,0:T(1,128)}, f32[36,1,128]{2,1,0:T(1,128)}) custom-call(f32[6,4,16,128]{3,2,1,0:T(8,128)S(1)} %get-tuple-element.15.refs_0_, f32[12,4,16,128]{3,2,1,0:T(8,128)S(1)} %get-tuple-element.16.refs_1_, ...), custom_call_target="tpu_custom_call" | custom-call | tf_op jit(solution)/shard_map/pallas_call | solution.py:638
